TPU v7x, 512 devices: a whole 4x8x8 slice. The times are simulated.
512 devices in a mesh: region: 32 (over y, x_lo, core), grp: 16 (over z, x_hi).
Axes of the slice: x: 4 (x_hi: 2, x_lo: 2; x = x_hi * 2 + x_lo), y: 8, z: 8, core: 2. Of those that a mesh axis runs over, the one named last changes fastest.
Arguments:
- transmission: float32 [2, 640, 20480], P(None, 'grp', 'region'), may hold values from -3 to 3
- probe: bfloat16 [2, 8, 512, 512], P(None, None, 'grp'), may hold values from -1.5 to 1.5
- measured: float32 [32, 512, 512], P('region', 'grp'), may hold values from 0 to 2
- positions: int32 [32, 2], P('region'), may hold values from 0 to 128
- past_steps: float32 [4, 2, 640, 20480], P(None, None, 'grp', 'region'), may hold values from -40 to 40
- past_changes: float32 [3, 2, 640, 20480], P(None, None, 'grp', 'region'), may hold values from -240 to 240
- old_gradient: float32 [2, 640, 20480], P(None, 'grp', 'region'), may hold values from -40 to 40
Outputs:
- updated: float32 [2, 640, 20480], P(None, 'grp', 'region')
- gradient: float32 [2, 640, 20480], P(None, 'grp', 'region')
All inputs are finite; a program needn't handle non-finite values.
Results may differ from a plain program's by a relative error of at most 0.019.
The roundings to bfloat16 on the way count: a program that leaves them out, or rounds other values in their place, can miss the bound.
Values may be sent and summed in bfloat16 or wider, within the bound.
A program may use at most 64 MiB of HBM per device.

v0:
```python
import math

import jax
import jax.numpy as jnp
from jax import lax
from jax.sharding import PartitionSpec as P

TWO_PI = 2.0 * math.pi
CURVE_FLOOR = 0.25
TIKHONOV = 0.5
EPSILON = 1e-06


def dft_tables(count):
    index = jnp.arange(count, dtype=jnp.int32)
    phase = (index[:, None] * index[None, :] % count).astype(jnp.float32) * (TWO_PI / count)
    factor = 1.0 / math.sqrt(count)
    return (
        (jnp.cos(phase) * factor).astype(jnp.bfloat16),
        (-jnp.sin(phase) * factor).astype(jnp.bfloat16),
    )


def chirp_table(count):
    index = jnp.arange(count, dtype=jnp.int32)
    wavenumber = (index + count // 2) % count - count // 2
    phase = (wavenumber * wavenumber % (4 * count)).astype(jnp.float32) * (TWO_PI / (4 * count))
    return (jnp.cos(phase), -jnp.sin(phase))


def rotate(real_part, imag_part, turn_real, turn_imag):
    return (
        real_part * turn_real - imag_part * turn_imag,
        real_part * turn_imag + imag_part * turn_real,
    )


def narrow(pair):
    return jnp.stack([pair[0], pair[1]]).astype(jnp.bfloat16)


def right_product(field, matrix_real, matrix_imag):

    def single(left, right):
        return jnp.einsum("...k,kj->...j", left, right, preferred_element_type=jnp.float32)

    return (
        single(field[0], matrix_real) - single(field[1], matrix_imag),
        single(field[0], matrix_imag) + single(field[1], matrix_real),
    )


def left_product(matrix_real, matrix_imag, field):

    def single(left, right):
        return jnp.einsum("jk,...kc->...jc", left, right, preferred_element_type=jnp.float32)

    return (
        single(matrix_real, field[0]) - single(matrix_imag, field[1]),
        single(matrix_real, field[1]) + single(matrix_imag, field[0]),
    )


def shards(transmission, probe, measured, positions, past_steps, past_changes, old_gradient):
    member = lax.axis_index("grp")
    frame_len = probe.shape[3]
    rows_here = probe.shape[2]
    tile_len = transmission.shape[2]
    anchor = jnp.zeros((), jnp.int32)
    fwd_real, fwd_imag = dft_tables(frame_len)
    inv_imag = -fwd_imag
    chirp_real, chirp_imag = chirp_table(frame_len)
    probe_wide = probe.astype(jnp.float32)
    tile = lax.all_gather(transmission.astype(jnp.bfloat16), "grp", axis=1, tiled=True)
    frame = 0
    first_row = positions[frame, 0] + member * rows_here
    window = jnp.swapaxes(
        lax.dynamic_slice(
            tile, (anchor, positions[frame, 1], first_row), (2, frame_len, rows_here)
        ),
        1,
        2,
    ).astype(jnp.float32)
    wave = narrow(rotate(probe_wide[0], probe_wide[1], window[0], window[1]))
    section = narrow(rotate(*right_product(wave, fwd_real, fwd_imag), chirp_real, chirp_imag))
    spread = narrow(right_product(section, fwd_real, inv_imag))
    section = narrow(
        rotate(
            *left_product(
                fwd_real,
                fwd_imag,
                lax.all_to_all(spread, "grp", split_axis=3, concat_axis=2, tiled=True),
            ),
            chirp_real[:, None],
            chirp_imag[:, None]
        )
    )
    far_field = narrow(left_product(fwd_real, inv_imag, section))
    near_rows = lax.all_to_all(far_field, "grp", split_axis=2, concat_axis=3, tiled=True)
    field_wide = near_rows.astype(jnp.float32)
    misfit = (
        jnp.sum(field_wide[0] * field_wide[0] + field_wide[1] * field_wide[1], axis=0)
        - measured[frame]
    )
    weighted = (misfit * field_wide).astype(jnp.bfloat16)
    section = narrow(
        rotate(
            *left_product(
                fwd_real,
                fwd_imag,
                lax.all_to_all(weighted, "grp", split_axis=3, concat_axis=2, tiled=True),
            ),
            chirp_real[:, None],
            -chirp_imag[:, None]
        )
    )
    returned = narrow(left_product(fwd_real, inv_imag, section))
    section = narrow(
        rotate(
            *right_product(
                lax.all_to_all(returned, "grp", split_axis=2, concat_axis=3, tiled=True),
                fwd_real,
                fwd_imag,
            ),
            chirp_real,
            -chirp_imag
        )
    )
    back_wave = jnp.stack(right_product(section, fwd_real, inv_imag))
    grad_real = 4.0 * jnp.sum(probe_wide[0] * back_wave[0] + probe_wide[1] * back_wave[1], axis=0)
    grad_imag = 4.0 * jnp.sum(probe_wide[0] * back_wave[1] - probe_wide[1] * back_wave[0], axis=0)
    frame_grads = [jnp.stack([grad_real, grad_imag])]
    scattered = jnp.zeros((2, tile_len, tile_len), jnp.float32)
    frame = 0
    corner = (anchor, positions[frame, 1], positions[frame, 0] + member * rows_here)
    scattered = lax.dynamic_update_slice(scattered, jnp.swapaxes(frame_grads[frame], 1, 2), corner)
    data_grad = lax.psum_scatter(
        scattered.astype(jnp.bfloat16), "grp", scatter_dimension=1, tiled=True
    ).astype(jnp.float32)
    gradient = data_grad + TIKHONOV * transmission
    depth = past_steps.shape[0]
    last = depth - 1
    change_new = gradient - old_gradient
    steps_list = [past_steps[index] for index in range(depth)]
    changes = [past_changes[index] for index in range(depth - 1)] + [change_new]
    alphas = [None] * depth
    curvature, self_dots, change_norm = lax.psum(
        (
            jnp.stack([jnp.sum(steps_list[index] * changes[index]) for index in range(depth)]),
            jnp.sum(past_steps * past_steps, axis=(1, 2, 3)),
            jnp.sum(change_new * change_new),
        ),
        ("region", "grp"),
    )
    weights = [
        1.0 / jnp.maximum(curvature[index], CURVE_FLOOR * self_dots[index])
        for index in range(depth)
    ]
    direction = gradient
    for index in reversed(range(depth)):
        alphas[index] = weights[index] * lax.psum(
            jnp.sum(steps_list[index] * direction), ("region", "grp")
        )
        direction = direction - alphas[index] * changes[index]
    scale = jnp.maximum(curvature[last], CURVE_FLOOR * self_dots[last]) / (change_norm + EPSILON)
    direction = scale * direction
    for index in range(depth):
        beta = weights[index] * lax.psum(jnp.sum(changes[index] * direction), ("region", "grp"))
        direction = direction + (alphas[index] - beta) * steps_list[index]
    return (transmission - direction, gradient)


def solution(mesh):
    return jax.shard_map(
        shards,
        mesh=mesh,
        in_specs=(
            P(None, "grp", "region"),
            P(None, None, "grp", None),
            P("region", "grp", None),
            P("region", None),
            P(None, None, "grp", "region"),
            P(None, None, "grp", "region"),
            P(None, "grp", "region"),
        ),
        out_specs=(P(None, "grp", "region"), P(None, "grp", "region")),
        check_vma=False,
    )
```

profile of v0, /device:TPU:1, one launch (start us, length us, event | category | flops | bytes accessed | tf_op | source)
XLA Modules:
  0.0 1376.2 jit_solution(13313109563345839940)
XLA Ops:
  13.6 88.9 %all-gather.2.cloned.1.call-done = bf16[2,640,640]{2,1,0:T(8,128)(2,1)} async-done(((bf16[2,40,640]{2,1,0:T(8,128)(2,1)}), bf16[2,640,640]{2,1,0:T(8,128)(2,1)}) %all-gather.2.cloned.1.call-update) | async-done | bytes 1638416 | tf_op jit(solution)/shard_map/all_gather | solution.py:74
  104.3 4.4 fusion.71
  108.7 4.5 fusion.42
  113.2 4.5 convolution_subtract_fusion.7
  117.7 4.8 add_convert_fusion.3
  122.4 4.4 fusion.68
  126.9 4.5 fusion.32
  131.3 5.0 fusion.13
  136.4 4.7 fusion.12
  141.9 2.9 copy.26
  144.8 2.7 reshape.161
  147.5 18.9 %all_to_all.54 = bf16[16,2,8192]{2,1,0:T(2,128)(2,1)} all-to-all(bf16[16,2,8192]{2,1,0:T(2,128)(2,1)} %reshape.161), channel_id=1, replica_groups=mesh['region'=32,'grp'=16] {'grp'}, dimensions={0} | all-to-all | bytes 1048576 | tf_op jit(solution)/shard_map/all_to_all | solution.py:92
  166.3 3.1 reshape.162
  172.1 5.3 fusion.63
  178.5 4.4 fusion.65
  182.9 4.5 convolution_add_fusion.5
  187.4 4.8 fusion.84
  192.2 15.0 %fusion.61 = f32[8,32,512]{2,1,0:T(8,128)S(1)} fusion(bf16[8,512,32]{1,2,0:T(8,128)(2,1)S(1)} %get-tuple-element.35), kind=kOutput, calls=%fused_computation.97 | convolution fusion | flops 138412032 | bytes 786432 | tf_op jit(solution)/shard_map/jk,...kc->...jc/dot_general | solution.py:56
  207.2 4.4 fusion.59
  211.7 4.7 fusion.11
  216.4 4.7 fusion.10
  222.0 2.9 copy.28
  224.9 2.7 reshape.163
  227.5 18.5 %all_to_all.55 = bf16[16,2,8192]{2,1,0:T(2,128)(2,1)} all-to-all(bf16[16,2,8192]{2,1,0:T(2,128)(2,1)} %reshape.163), channel_id=1, replica_groups=mesh['region'=32,'grp'=16] {'grp'}, dimensions={0} | all-to-all | bytes 1048576 | tf_op jit(solution)/shard_map/all_to_all | solution.py:99
  246.0 3.1 reshape.164
  249.1 3.1 copy.46
  252.2 3.5 convert_element_type.237
  259.5 2.9 copy.30
  262.4 2.7 reshape.165
  265.0 4.4 all-to-all-start.2
  269.5 13.4 all-to-all-done.2
  283.0 3.3 reshape.166
  286.2 3.3 copy.37
  289.5 3.0 fusion.281
  296.0 5.3 fusion.55
  303.9 4.4 fusion.57
  308.3 4.5 convolution_add_fusion.3
  312.8 5.2 fusion.86
  318.0 4.4 fusion.53
  322.4 4.4 fusion.51
  326.8 4.7 fusion.9
  331.6 4.7 fusion.8
  337.2 2.9 copy.34
  340.1 2.7 reshape.167
  342.7 17.8 %all_to_all.56 = bf16[16,2,8192]{2,1,0:T(2,128)(2,1)} all-to-all(bf16[16,2,8192]{2,1,0:T(2,128)(2,1)} %reshape.167), channel_id=1, replica_groups=mesh['region'=32,'grp'=16] {'grp'}, dimensions={0} | all-to-all | bytes 1048576 | tf_op jit(solution)/shard_map/all_to_all | solution.py:121
  360.5 3.1 reshape.168
  366.3 4.4 fusion.49
  370.7 5.4 fusion.35
  377.1 4.5 convolution_subtract_fusion.1
  381.6 4.8 add_convert_fusion
  386.4 4.6 fusion.46
  391.0 4.5 fusion.25
  395.5 4.5 convolution_subtract_fusion
  400.0 4.8 fusion.22
  405.1 4.5 dynamic_update_slice.3
  413.0 164.3 %reduce-scatter.4.cloned.1.call-done = bf16[40,1280]{1,0:T(8,128)(2,1)} async-done(((bf16[640,1280]{1,0:T(8,128)(2,1)}), bf16[40,1280]{1,0:T(8,128)(2,1)}) %reduce-scatter.4.cloned.1.call-update) | async-done | bytes 102416
  581.6 100.6 %all-reduce.1 = (f32[4]{0:T(128)S(1)}, f32[4]{0:T(128)S(1)}, f32[]{:T(128)}) all-reduce(f32[4]{0:T(128)S(1)} %pad_maximum_fusion.4, f32[4]{0:T(128)S(1)} %multiply_reduce_fusion, f32[]{:T(128)} %get-tuple-element.7), channel_id=1, replica_groups=mesh['region'=32,'grp'=16] {'region','grp'}, use_global_device_ids=true, to_apply=%region_8.9 | all-reduce | flops 9 | bytes 72 | tf_op jit(solution)/shard_map/psum | solution.py:147
  686.1 95.7 %psum.81 = f32[]{:T(128)} all-reduce(f32[]{:T(128)} %fusion.95), channel_id=1, replica_groups=mesh['region'=32,'grp'=16] {'region','grp'}, use_global_device_ids=true, to_apply=%region_16.17 | all-reduce | flops 1 | bytes 8 | tf_op jit(solution)/shard_map/psum | solution.py:161
  784.3 94.4 %psum.82 = f32[]{:T(128)} all-reduce(f32[]{:T(128)} %get-tuple-element.19), channel_id=1, replica_groups=mesh['region'=32,'grp'=16] {'region','grp'}, use_global_device_ids=true, to_apply=%region_18.19 | all-reduce | flops 1 | bytes 8 | tf_op jit(solution)/shard_map/psum | solution.py:161
  881.3 96.2 %all-reduce = (f32[]{:T(128)}, f32[]{:T(128)}) all-reduce(f32[]{:T(128)} %fusion.106, f32[]{:T(128)} %get-tuple-element.9), channel_id=1, replica_groups=mesh['region'=32,'grp'=16] {'region','grp'}, use_global_device_ids=true, to_apply=%region_20.21 | all-reduce | flops 2 | bytes 16 | tf_op jit(solution)/shard_map/psum | solution.py:161
  980.8 95.2 %psum.84 = f32[]{:T(128)} all-reduce(f32[]{:T(128)} %get-tuple-element.17), channel_id=1, replica_groups=mesh['region'=32,'grp'=16] {'region','grp'}, use_global_device_ids=true, to_apply=%region_22.23 | all-reduce | flops 1 | bytes 8 | tf_op jit(solution)/shard_map/psum | solution.py:168
  1077.4 96.0 %psum.85 = f32[]{:T(128)} all-reduce(f32[]{:T(128)} %fusion.99), channel_id=1, replica_groups=mesh['region'=32,'grp'=16] {'region','grp'}, use_global_device_ids=true, to_apply=%region_24.25 | all-reduce | flops 1 | bytes 8 | tf_op jit(solution)/shard_map/psum | solution.py:168
  1174.8 95.5 %psum.86 = f32[]{:T(128)} all-reduce(f32[]{:T(128)} %get-tuple-element.15), channel_id=1, replica_groups=mesh['region'=32,'grp'=16] {'region','grp'}, use_global_device_ids=true, to_apply=%region_26.27 | all-reduce | flops 1 | bytes 8 | tf_op jit(solution)/shard_map/psum | solution.py:168
  1271.7 95.9 %psum.87 = f32[]{:T(128)} all-reduce(f32[]{:T(128)} %multiply_reduce_fusion.1), channel_id=1, replica_groups=mesh['region'=32,'grp'=16] {'region','grp'}, use_global_device_ids=true, to_apply=%region_28.29 | all-reduce | flops 1 | bytes 8 | tf_op jit(solution)/shard_map/psum | solution.py:168
  (72 shorter events, 40.3 us)
Async XLA Ops:
  7.2 95.4 %all-gather.2.cloned.1.call-start = ((), (), s32[]{:S(2)}) async-start(), calls=%async_computation.5 | async-start | bytes 1740800 | tf_op jit(solution)/shard_map/all_gather | solution.py:74
  178.5 4.4 copy-start.7
  255.8 2.8 copy-start.5
  265.0 17.9 %all-to-all-start.2 = ((bf16[16,2,8192]{2,1,0:T(2,128)(2,1)}), bf16[16,2,8192]{2,1,0:T(2,128)(2,1)}, u32[]{:S(2)}, u32[]{:S(2)}) async-start(bf16[16,2,8192]{2,1,0:T(2,128)(2,1)} %reshape.165), calls=%async_computation.2 | async-start | bytes 1048576 | tf_op jit(solution)/shard_map/all_to_all | solution.py:111
  269.4 307.9 %reduce-scatter.4.cloned.1.call-start = ((), (), s32[]{:S(2)}) async-start(), calls=%async_computation.6 | async-start | bytes 1740800
  303.9 4.4 copy-start.6
  377.1 4.5 copy-start.8
  411.3 1.5 copy-start
  412.8 165.5 %copy-start.1 = (f32[3,2,40,640]{3,2,1,0:T(8,128)S(1)}, f32[3,2,40,640]{3,2,1,0:T(8,128)}, u32[]{:S(2)}) copy-start(f32[3,2,40,640]{3,2,1,0:T(8,128)} %param.12) | copy-start | bytes 1843204
  412.8 165.5 %copy-start.2 = (f32[2,40,640]{2,1,0:T(8,128)S(1)}, f32[2,40,640]{2,1,0:T(8,128)}, u32[]{:S(2)}) copy-start(f32[2,40,640]{2,1,0:T(8,128)} %param.7) | copy-start | bytes 614404
  412.8 165.5 %copy-start.4 = (f32[2,40,640]{2,1,0:T(8,128)S(1)}, f32[2,40,640]{2,1,0:T(8,128)}, u32[]{:S(2)}) copy-start(f32[2,40,640]{2,1,0:T(8,128)} %param.13) | copy-start | bytes 614404
  579.1 595.7 %copy-start.3 = (f32[2,40,640]{2,1,0:T(8,128)}, f32[2,40,640]{2,1,0:T(8,128)S(1)}, u32[]{:S(2)}) copy-start(f32[2,40,640]{2,1,0:T(8,128)S(1)} %get-tuple-element.22) | copy-start | bytes 614404
Sparse Core Ops, SparseCore 0:
  11.8 90.7 all-gather.1
  412.9 164.3 reduce-scatter.3
where the time goes:
time: 1390 us; the launch traced here: 1380 us
  blocking collectives  825 us (59%)
  waiting for transfers between devices  267 us (19%)
  matrix products  160 us (12%)
  local copies, waits for them, and re-layouts  72.8 us (5%)
  between operations  28.3 us (2%)
  other arithmetic  19.4 us (1%)
    psum x4, blocking collectives, shards(): lax.psum(jnp.sum(changes[index] * direction), ('region', 'grp'))  383 us
    psum x3, blocking collectives, shards(): lax.psum(jnp.sum(steps_list[index] * direction), ('region', 'grp'))  286 us
    unnamed x3, waiting for transfers between devices  164 us
    psum x1, blocking collectives, shards(): lax.psum((jnp.stack([jnp.sum(steps_list[index] * changes[index]) for inde...  101 us
    all_gather x1, waiting for transfers between devices, shards(): lax.all_gather(transmission.astype(jnp.bfloat16), 'grp', axis=1, tiled=True)  88.9 us
    dot_general x16, matrix products, single(): jnp.einsum('jk,...kc->...jc', left, right, preferred_element_type=jnp.flo...  85.7 us
    dot_general x16, matrix products, single(): jnp.einsum('...k,kj->...j', left, right, preferred_element_type=jnp.float32)  74.2 us
  transfers between devices with their start and end apart: 3, of which 3 were waited for; matrix products, arithmetic and copies ran while one was open for 0% of the time, Pallas kernels for 0%

commit v1 on v0

v1 whole, which is shorter than its diff:
```python
import functools

import jax
import jax.numpy as jnp
import ml_dtypes
import numpy as np
from jax import lax
from jax.experimental import pallas as pl
from jax.experimental.pallas import tpu as pltpu
from jax.sharding import PartitionSpec as P

CURVE_FLOOR = 0.25
TIKHONOV = 0.5
EPSILON = 1e-06
F32 = jnp.float32
BF16 = jnp.bfloat16
LANES = 128


def propagator(count):
    index = np.arange(count)
    phase = np.outer(index, index) % count * (2.0 * np.pi / count)
    factor = 1.0 / np.sqrt(count)
    real = (np.cos(phase) * factor).astype(np.float32).astype(ml_dtypes.bfloat16)
    imag = (-np.sin(phase) * factor).astype(np.float32).astype(ml_dtypes.bfloat16)
    table = real.astype(np.float64) + 1j * imag.astype(np.float64)
    wavenumber = (index + count // 2) % count - count // 2
    chirp = np.exp(-2j * np.pi * (wavenumber * wavenumber % (4 * count)) / (4 * count))
    folded = (table * chirp[None, :]) @ table.conj()
    return np.stack([folded.real, folded.imag]).astype(np.float32).astype(ml_dtypes.bfloat16)


def dot(left, right):
    return jnp.dot(left, right, preferred_element_type=F32)


def dot_t(left, right):
    return lax.dot_general(left, right, (((1,), (1,)), ((), ())), preferred_element_type=F32)


def iota(shape, dim):
    return lax.broadcasted_iota(jnp.int32, shape, dim)


def quad(parts):
    lane = iota(parts[0].shape, 1)
    low = lane % 128 < 64
    even = lane % 64 < 32
    roll = lambda x, s: pltpu.roll(x, s, 1)
    a0 = jnp.where(low, parts[0], roll(parts[2], 64))
    a2 = jnp.where(low, roll(parts[0], 64), parts[2])
    a1 = jnp.where(low, parts[1], roll(parts[3], 64))
    a3 = jnp.where(low, roll(parts[1], 64), parts[3])
    return [
        jnp.where(even, a0, roll(a1, 32)),
        jnp.where(even, roll(a0, 96), a1),
        jnp.where(even, a2, roll(a3, 32)),
        jnp.where(even, roll(a2, 96), a3),
    ]


def spread_sum(x):
    x = x + pltpu.roll(x, 64, 1)
    return x + pltpu.roll(x, 32, 1)


def barrier(axis, size, also=()):
    sem = pltpu.get_barrier_semaphore()
    total = 0
    for name, count in ((axis, size), *also):
        me = lax.axis_index(name)

        def signal(k, carry, name=name, count=count, me=me):
            pl.semaphore_signal(
                sem,
                inc=1,
                device_id={name: lax.rem(me + k, count)},
                device_id_type=pl.DeviceIdType.MESH,
            )
            return carry

        lax.fori_loop(1, count, signal, 0)
        total += count - 1
    pl.semaphore_wait(sem, total)


def exchange(axis, size, src, dst, send, recv):
    me = lax.axis_index(axis)

    def copy(peer, slot):
        return pltpu.make_async_remote_copy(
            src_ref=src(peer),
            dst_ref=dst(slot),
            send_sem=send.at[peer],
            recv_sem=recv.at[slot],
            device_id={axis: peer},
            device_id_type=pl.DeviceIdType.MESH,
        )

    def start():
        def one(k, carry):
            copy(lax.rem(me + k, size), me).start()
            return carry

        lax.fori_loop(1, size, one, 0)

    def wait_recv():
        def one(k, carry):
            peer = lax.rem(me + k, size)
            copy(peer, peer).wait_recv()
            return carry

        lax.fori_loop(1, size, one, 0)

    def wait_send():
        def one(k, carry):
            copy(lax.rem(me + k, size), me).wait_send()
            return carry

        lax.fori_loop(1, size, one, 0)

    return start, wait_recv, wait_send


def frame_kernel(
    grp,
    pos,
    trans_hbm,
    probe_hbm,
    meas_hbm,
    k_hbm,
    out_ref,
    trans,
    probe,
    meas,
    kmat,
    x_send,
    x_recv,
    m_send,
    m_recv,
    f_send,
    f_recv,
    b_send,
    b_recv,
    g_send,
    g_recv,
    select,
    target,
    field,
    tile,
    load_sem,
    send_sem,
    recv_sem,
):
    me = lax.axis_index("grp")
    cols, length = trans.shape[1], trans.shape[2]
    modes, rows, n = probe.shape[1], probe.shape[2], probe.shape[3]
    tiles = n // LANES
    halves = modes // 4
    loads = [
        pltpu.make_async_copy(src, dst, load_sem.at[i])
        for i, (src, dst) in enumerate(
            ((trans_hbm, trans), (meas_hbm, meas), (probe_hbm, probe), (k_hbm, kmat))
        )
    ]
    for load in loads:
        load.start()
    row0, col0 = pos[0, 0], pos[0, 1]
    mine = lambda size: pl.ds(pl.multiple_of(me * size, size), size)

    loads[0].wait()
    gap = jnp.zeros((LANES // 2 - cols, length), F32)
    block = jnp.concatenate([trans[0], gap, trans[1], gap], axis=0).astype(BF16)
    pick = iota((n, length), 1) == iota((n, length), 0) + row0
    x_send[...] = dot_t(pick.astype(F32).astype(BF16), block).astype(BF16)
    x_recv[me] = x_send[mine(rows), :]

    loads[1].wait()
    for t in range(tiles):
        packed = quad([meas[0, 8 * a : 8 * a + 8, LANES * t : LANES * (t + 1)] for a in range(4)])
        for g in range(4):
            m_send[4 * t + g] = packed[g]
    m_recv[me] = m_send[me]

    barrier("grp", grp)
    x_copy = exchange(
        "grp",
        grp,
        lambda p: x_send.at[pl.ds(pl.multiple_of(p * rows, rows), rows), :],
        lambda s: x_recv.at[s],
        send_sem.at[0],
        recv_sem.at[0],
    )
    m_copy = exchange(
        "grp", grp, lambda p: m_send.at[p], lambda s: m_recv.at[s], send_sem.at[1], recv_sem.at[1]
    )
    x_copy[0]()
    m_copy[0]()

    for d in range(grp):
        lane = iota((n, LANES), 1) % (LANES // 2)
        hit = (lane + cols * d == iota((n, LANES), 0) + col0) & (lane < cols)
        select[:, LANES * d : LANES * (d + 1)] = hit.astype(F32).astype(BF16)
    loads[2].wait()
    loads[3].wait()
    x_copy[1]()
    first = iota((rows, LANES), 1) < LANES // 2
    stacked = []
    for d in range(grp):
        x = x_recv[d].astype(F32)
        zero = jnp.zeros_like(x)
        stacked.append(
            jnp.concatenate([jnp.where(first, x, zero), jnp.where(first, zero, x), zero, zero], axis=0).astype(BF16)
        )
    window = jnp.transpose(dot_t(select[...], jnp.concatenate(stacked, axis=1)))
    win_r, win_i = window[:rows], window[rows : 2 * rows]

    k_r, k_i = kmat[0], kmat[1]
    f_copies, b_copies = [], []
    for q in range(halves):
        wave_r, wave_i = [], []
        for m in range(4 * q, 4 * q + 4):
            p_r, p_i = probe[0, m].astype(F32), probe[1, m].astype(F32)
            wave_r.append(p_r * win_r - p_i * win_i)
            wave_i.append(p_r * win_i + p_i * win_r)
        wave_r = jnp.concatenate(wave_r, axis=0).astype(BF16)
        wave_i = jnp.concatenate(wave_i, axis=0).astype(BF16)
        out = (
            dot(wave_r, k_r) - dot(wave_i, k_i),
            dot(wave_r, k_i) + dot(wave_i, k_r),
        )
        for c in range(2):
            for t in range(tiles):
                packed = quad(
                    [out[c][rows * m : rows * (m + 1), LANES * t : LANES * (t + 1)] for m in range(4)]
                )
                for g in range(4):
                    f_send[q, 4 * t + g, :, LANES * c : LANES * (c + 1)] = packed[g].astype(BF16)
        f_recv[q, me] = f_send[q, me]
        f_copies.append(
            exchange(
                "grp",
                grp,
                lambda p, q=q: f_send.at[q, p],
                lambda s, q=q: f_recv.at[q, s],
                send_sem.at[2 + q],
                recv_sem.at[2 + q],
            )
        )
        f_copies[q][0]()

    m_copy[1]()
    packed = m_recv[...].reshape(grp * 8, LANES)
    group = iota((grp * 8, LANES), 1) // 32
    for a in range(4):
        spread = spread_sum(jnp.where(group == a, packed, jnp.zeros_like(packed)))
        target[:, a] = spread.reshape(grp, 8, LANES)

    intensity = jnp.zeros((n, LANES), F32)
    for q in range(halves):
        f_copies[q][1]()
        x = f_recv[q].reshape(n, 2 * LANES)
        by_r, by_i = dot(k_r, x), dot(k_i, x)
        d_r = (by_r[:, :LANES] - by_i[:, LANES:]).astype(BF16)
        d_i = (by_r[:, LANES:] + by_i[:, :LANES]).astype(BF16)
        field[q, :, :LANES] = d_r
        field[q, :, LANES:] = d_i
        d_r, d_i = d_r.astype(F32), d_i.astype(F32)
        intensity = intensity + (d_r * d_r + d_i * d_i)
    misfit = spread_sum(intensity) - target[...].reshape(n, LANES)
    for q in range(halves):
        e_r = (misfit * field[q, :, :LANES].astype(F32)).astype(BF16)
        e_i = (misfit * field[q, :, LANES:].astype(F32)).astype(BF16)
        e = jnp.concatenate([e_r, e_i], axis=1)
        by_r, by_i = dot(k_r, e), dot(k_i, e)
        b_send[q, :, :, :LANES] = (by_r[:, :LANES] + by_i[:, LANES:]).astype(BF16).reshape(grp, rows, LANES)
        b_send[q, :, :, LANES:] = (by_r[:, LANES:] - by_i[:, :LANES]).astype(BF16).reshape(grp, rows, LANES)
        b_recv[q, me] = b_send[q, me]
        b_copies.append(
            exchange(
                "grp",
                grp,
                lambda p, q=q: b_send.at[q, p],
                lambda s, q=q: b_recv.at[q, s],
                send_sem.at[2 + halves + q],
                recv_sem.at[2 + halves + q],
            )
        )
        b_copies[q][0]()

    grad_r = jnp.zeros((rows, n), F32)
    grad_i = jnp.zeros((rows, n), F32)
    for q in range(halves):
        b_copies[q][1]()
        back = []
        for c in range(2):
            by_tile = []
            for t in range(tiles):
                packed = quad(
                    [b_recv[q, 4 * t + g, :, LANES * c : LANES * (c + 1)].astype(F32) for g in range(4)]
                )
                by_tile.append(jnp.concatenate(packed, axis=0))
            back.append(jnp.concatenate(by_tile, axis=1).astype(BF16))
        p_r = dot(back[0], k_r) + dot(back[1], k_i)
        p_i = dot(back[1], k_r) - dot(back[0], k_i)
        for m in range(4):
            w_r, w_i = probe[0, 4 * q + m].astype(F32), probe[1, 4 * q + m].astype(F32)
            o_r, o_i = p_r[rows * m : rows * (m + 1)], p_i[rows * m : rows * (m + 1)]
            grad_r = grad_r + (w_r * o_r + w_i * o_i)
            grad_i = grad_i + (w_r * o_i - w_i * o_r)

    grad_r = (4.0 * grad_r).astype(BF16)
    grad_i = (4.0 * grad_i).astype(BF16)
    place = iota((length, n), 0) == iota((length, n), 1) + col0
    tall = dot_t(
        place.astype(F32).astype(BF16), jnp.concatenate([grad_r] * 4 + [grad_i] * 4, axis=0)
    )
    tall = tall.reshape(grp, cols // 8, 8, 2 * LANES)
    parts = [
        tall[:, j, :, LANES * c : LANES * (c + 1)] for c in range(2) for j in range(cols // 8)
    ]
    group = iota((grp, 8, LANES), 2) // 32
    zero = jnp.zeros((grp, 8, LANES), F32)
    wide = []
    for w in range(4):
        value = zero
        for p in range(4):
            if 4 * w + p < len(parts):
                value = jnp.where(group == p, parts[4 * w + p], value)
        wide.append(value)
    g_send[...] = jnp.concatenate(wide, axis=1).astype(BF16)
    g_recv[me] = g_send[me]
    g_copy = exchange(
        "grp",
        grp,
        lambda p: g_send.at[p],
        lambda s: g_recv.at[s],
        send_sem.at[2 + 2 * halves],
        recv_sem.at[2 + 2 * halves],
    )
    g_copy[0]()
    put = (iota((n, length), 1) == iota((n, length), 0) + row0).astype(F32).astype(BF16)
    g_copy[1]()
    for t in range(tiles):
        whole = [g_recv[4 * t + g].astype(F32) for g in range(4)]
        for w in range((len(parts) + 3) // 4):
            packed = quad([x[8 * w : 8 * w + 8] for x in whole])
            for p in range(4):
                if 4 * w + p < len(parts):
                    at = 8 * (4 * w + p)
                    tile[at : at + 8, LANES * t : LANES * (t + 1)] = packed[p]
    out = dot(tile[...].astype(BF16), put)
    out_ref[0] = out[:cols]
    out_ref[1] = out[cols:]

    for copies in (x_copy, m_copy, *f_copies, *b_copies, g_copy):
        copies[2]()


def update_kernel(
    grp,
    region,
    data_ref,
    trans_ref,
    steps_ref,
    changes_ref,
    old_ref,
    updated_ref,
    gradient_ref,
    change,
    gram,
    one_send,
    one_recv,
    two_recv,
    one_send_sem,
    one_recv_sem,
    two_send_sem,
    two_recv_sem,
):
    depth = steps_ref.shape[0]
    last = depth - 1
    cols, length = trans_ref.shape[1], trans_ref.shape[2]
    strips = [(c, j) for c in range(2) for j in range(cols // 8)]
    names = []
    for i in range(depth):
        names += [("ss", i, i), ("sg", i, i), ("yg", i, i)]
        for j in range(i, depth):
            names += [("sy", i, j), ("yy", i, j)]
    slot = {name: number for number, name in enumerate(names)}
    gram[...] = jnp.zeros_like(gram)
    for c, j in strips:
        at = (c, slice(8 * j, 8 * j + 8), slice(None))
        grad = data_ref[at] + TIKHONOV * trans_ref[at]
        gradient_ref[at] = grad
        new = grad - old_ref[at]
        change[at] = new
        s = [steps_ref[(i, *at)] for i in range(depth)]
        y = [changes_ref[(i, *at)] for i in range(depth - 1)] + [new]
        for (kind, a, b), number in slot.items():
            left = {"ss": s, "sg": s, "yg": y, "sy": s, "yy": y}[kind][a]
            right = {"ss": s, "sg": [grad] * depth, "yg": [grad] * depth, "sy": y, "yy": y}[kind][b]
            product = left * right
            gram[number] += sum(product[:, LANES * t : LANES * (t + 1)] for t in range(length // LANES))
    totals = jnp.sum(jnp.sum(gram[...], axis=1), axis=1, keepdims=True)
    group = iota((8, LANES), 1) // 32
    value = jnp.zeros((8, LANES), F32)
    for w in range(4):
        value = jnp.where(group == w, totals[8 * w : 8 * w + 8], value)
    one_send[0] = value

    barrier("grp", grp, (("region", region),))
    me, here = lax.axis_index("grp"), lax.axis_index("region")
    one_recv[me] = value
    one = exchange(
        "grp", grp, lambda p: one_send.at[0], lambda s: one_recv.at[s], one_send_sem, one_recv_sem
    )
    one[0]()
    one[1]()
    value = jnp.sum(one_recv[...], axis=0)
    one_send[1] = value
    two_recv[here] = value
    two = exchange(
        "region", region, lambda p: one_send.at[1], lambda s: two_recv.at[s], two_send_sem, two_recv_sem
    )
    two[0]()
    two[1]()
    value = jnp.sum(two_recv[...], axis=0)

    def inner(kind, a, b):
        number = slot[(kind, a, b)]
        at = 32 * (number // 8)
        return value[number % 8 : number % 8 + 1, at : at + 1]

    curve = [
        jnp.maximum(inner("sy", i, i), CURVE_FLOOR * inner("ss", i, i)) for i in range(depth)
    ]
    alphas = [None] * depth
    for i in reversed(range(depth)):
        along = inner("sg", i, i)
        for j in range(i + 1, depth):
            along = along - alphas[j] * inner("sy", i, j)
        alphas[i] = along / curve[i]
    scale = curve[last] / (inner("yy", last, last) + EPSILON)
    weights = []
    for i in range(depth):
        along = inner("yg", i, i)
        for j in range(depth):
            along = along - alphas[j] * inner("yy", min(i, j), max(i, j))
        along = scale * along
        for j in range(i):
            along = along + weights[j] * inner("sy", j, i)
        weights.append(alphas[i] - along / curve[i])
    alphas = [scale * alpha for alpha in alphas]
    for c, j in strips:
        at = (c, slice(8 * j, 8 * j + 8), slice(None))
        direction = scale * gradient_ref[at]
        for i in range(depth):
            y = change[at] if i == last else changes_ref[(i, *at)]
            direction = direction - alphas[i] * y + weights[i] * steps_ref[(i, *at)]
        updated_ref[at] = trans_ref[at] - direction
    one[2]()
    two[2]()


def shards(grp, region, transmission, probe, measured, positions, past_steps, past_changes, old_gradient):
    two, cols, length = transmission.shape
    _, modes, rows, n = probe.shape
    halves = modes // 4
    depth = past_steps.shape[0]
    phases = 3 + 2 * halves
    vmem = pl.BlockSpec(memory_space=pltpu.VMEM)
    hbm = pl.BlockSpec(memory_space=pl.ANY)
    data = pl.pallas_call(
        functools.partial(frame_kernel, grp),
        out_shape=jax.ShapeDtypeStruct((two, cols, length), F32),
        in_specs=[pl.BlockSpec(memory_space=pltpu.SMEM), hbm, hbm, hbm, hbm],
        out_specs=vmem,
        scratch_shapes=[
            pltpu.VMEM((two, cols, length), F32),
            pltpu.VMEM(probe.shape, BF16),
            pltpu.VMEM((1, rows, n), F32),
            pltpu.VMEM((2, n, n), BF16),
            pltpu.VMEM((n, LANES), BF16),
            pltpu.VMEM((grp, rows, LANES), BF16),
            pltpu.VMEM((grp, 8, LANES), F32),
            pltpu.VMEM((grp, 8, LANES), F32),
            pltpu.VMEM((halves, grp, rows, 2 * LANES), BF16),
            pltpu.VMEM((halves, grp, rows, 2 * LANES), BF16),
            pltpu.VMEM((halves, grp, rows, 2 * LANES), BF16),
            pltpu.VMEM((halves, grp, rows, 2 * LANES), BF16),
            pltpu.VMEM((grp, 32, LANES), BF16),
            pltpu.VMEM((grp, 32, LANES), BF16),
            pltpu.VMEM((n, grp * LANES), BF16),
            pltpu.VMEM((grp, 4, 8, LANES), F32),
            pltpu.VMEM((halves, n, 2 * LANES), BF16),
            pltpu.VMEM((two * cols, n), F32),
            pltpu.SemaphoreType.DMA((4,)),
            pltpu.SemaphoreType.DMA((phases, grp)),
            pltpu.SemaphoreType.DMA((phases, grp)),
        ],
        compiler_params=pltpu.CompilerParams(
            collective_id=0, has_side_effects=True, vmem_limit_bytes=48 << 20
        ),
        name="frame",
    )(positions, transmission, probe, measured, jnp.asarray(propagator(n)))
    shape = jax.ShapeDtypeStruct((two, cols, length), F32)
    return pl.pallas_call(
        functools.partial(update_kernel, grp, region),
        out_shape=(shape, shape),
        in_specs=[vmem] * 5,
        out_specs=(vmem, vmem),
        scratch_shapes=[
            pltpu.VMEM((two, cols, length), F32),
            pltpu.VMEM((32, 8, LANES), F32),
            pltpu.VMEM((2, 8, LANES), F32),
            pltpu.VMEM((grp, 8, LANES), F32),
            pltpu.VMEM((region, 8, LANES), F32),
            pltpu.SemaphoreType.DMA((grp,)),
            pltpu.SemaphoreType.DMA((grp,)),
            pltpu.SemaphoreType.DMA((region,)),
            pltpu.SemaphoreType.DMA((region,)),
        ],
        compiler_params=pltpu.CompilerParams(
            collective_id=1, has_side_effects=True, vmem_limit_bytes=32 << 20
        ),
        name="update",
    )(data, transmission, past_steps, past_changes, old_gradient)


def solution(mesh):
    return jax.shard_map(
        functools.partial(shards, mesh.shape["grp"], mesh.shape["region"]),
        mesh=mesh,
        in_specs=(
            P(None, "grp", "region"),
            P(None, None, "grp", None),
            P("region", "grp", None),
            P("region", None),
            P(None, None, "grp", "region"),
            P(None, None, "grp", "region"),
            P(None, "grp", "region"),
        ),
        out_specs=(P(None, "grp", "region"), P(None, "grp", "region")),
        check_vma=False,
    )
```

time: 1390 us -> 95 us (0.07)
  blocking collectives: 825 us -> 0 us
  waiting for transfers between devices: 267 us -> 0 us
  matrix products: 160 us -> 0 us
  Pallas kernels: 0 us -> 87.9 us
  local copies, waits for them, and re-layouts: 72.8 us -> 6.06 us
  between operations: 28.3 us -> 0.69 us
  other arithmetic: 19.4 us -> 0 us
    psum x8 -> x0, blocking collectives: 770 us -> none  [the longest x4 383 us: shards(): lax.psum(jnp.sum(changes[index] * direction), ('region', 'grp'))]
    unnamed x3 -> x0, waiting for transfers between devices: 164 us -> none
    dot_general x32 -> x0, matrix products: 160 us -> none  [the longest x16 85.7 us: single(): jnp.einsum('jk,...kc->...jc', left, right, preferred_element_type=jnp.flo...]
    all_gather x1 -> x0, waiting for transfers between devices: 88.9 us -> none  [shards(): lax.all_gather(transmission.astype(jnp.bfloat16), 'grp', axis=1, tiled=True)]
    pallas_call x0 -> x2, Pallas kernels: none -> 87.9 us  [the longest x1 60.6 us: shards(): pl.pallas_call(functools.partial(frame_kernel, grp), out_shape=jax.ShapeD...]
    all_to_all x3 -> x0, blocking collectives: 55.1 us -> none  [the longest x1 18.9 us: shards(): lax.all_to_all(spread, 'grp', split_axis=3, concat_axis=2, tiled=True)]
    unnamed x29 -> x18, local copies, waits for them, and re-layouts: 27.2 us -> 6.06 us
  transfers between devices with their start and end apart: 3 -> 0, of which waited for: 3 -> 0; matrix products, arithmetic and copies ran while one was open for 0% -> 0% of each run, Pallas kernels for 0% -> 0%
where the time goes in v1:
time: 95 us; the launch traced here: 94.7 us
  Pallas kernels  87.9 us (93%)
  local copies, waits for them, and re-layouts  6.06 us (6%)
    pallas_call x1, Pallas kernels, shards(): pl.pallas_call(functools.partial(frame_kernel, grp), out_shape=jax.ShapeD...  60.6 us
    pallas_call x1, Pallas kernels, shards(): pl.pallas_call(functools.partial(update_kernel, grp, region), out_shape=(...  27.3 us
    unnamed x18, local copies, waits for them, and re-layouts  6.06 us

profile of v1, /device:TPU:1, one launch (start us, length us, event | category | flops | bytes accessed | tf_op | source)
XLA Modules:
  0.0 94.7 jit_solution(1117154353042867417)
XLA Ops:
  0.6 0.0 copy-start
  0.6 1.2 %copy-done = bf16[2,512,512]{2,1,0:T(8,128)(2,1)S(1)} copy-done((bf16[2,512,512]{2,1,0:T(8,128)(2,1)S(1)}, bf16[2,512,512]{2,1,0:T(8,128)(2,1)}, u32[]{:S(2)}) %copy-start) | copy-done | bytes 1048600
  1.9 0.0 copy-start.2
  1.9 0.9 copy-done.2
  2.8 0.0 copy-start.4
  2.8 1.0 %copy-done.4 = bf16[2,8,32,512]{3,2,1,0:T(8,128)(2,1)S(1)} copy-done((bf16[2,8,32,512]{3,2,1,0:T(8,128)(2,1)S(1)}, bf16[2,8,32,512]{3,2,1,0:T(8,128)(2,1)}, u32[]{:S(2)}) %copy-start.4) | copy-done | bytes 524312
  3.8 0.0 copy-start.6
  3.8 0.8 copy-done.6
  4.7 0.0 copy-start.7
  4.7 0.7 copy-done.7
  5.3 0.0 copy-start.1
  5.3 0.0 copy-start.3
  5.3 0.0 copy-start.5
  5.3 60.6 %frame.1.data_ref = f32[2,40,640]{2,1,0:T(8,128)S(1)} custom-call(s32[1,2]{1,0:T(1,128)S(1)} %copy-done.7, f32[2,40,640]{2,1,0:T(8,128)S(1)} %copy-done.2, bf16[2,8,32,512]{3,2,1,0:T(8,128)(2,1)S(1)} %copy-done.4, f32[1,32,512]{2,1,0:T(8,128)S(1)} %copy-done.6, bf16[2,512,512]{2,1,0:T(8,128)(2,1)S(1)} %copy-done), custom_call_target="tpu_custom_call" | custom-call | tf_op jit(solution)/shard_map/frame/pallas_call | solution.py:473
  66.0 0.0 copy-done.1
  66.0 0.0 copy-done.3
  66.0 0.0 copy-done.5
  66.0 27.3 %update.1 = (f32[2,40,640]{2,1,0:T(8,128)S(1)}, f32[2,40,640]{2,1,0:T(8,128)S(1)}) custom-call(f32[2,40,640]{2,1,0:T(8,128)S(1)} %frame.1.data_ref, f32[2,40,640]{2,1,0:T(8,128)S(1)} %copy-done.2, f32[4,2,40,640]{3,2,1,0:T(8,128)S(1)} %copy-done.1, f32[3,2,40,640]{3,2,1,0:T(8,128)S(1)} %copy-done.3, f32[2,40,640]{2,1,0:T(8,128)S(1)} %copy-done.5), custom_call_target="tpu_custom_call" | custom-call | tf_op jit(solution)/shard_map/update/pallas_call | solution.py:507
  93.3 0.7 copy.12
  94.0 0.7 copy.13
Async XLA Ops:
  0.6 1.2 %copy-start = (bf16[2,512,512]{2,1,0:T(8,128)(2,1)S(1)}, bf16[2,512,512]{2,1,0:T(8,128)(2,1)}, u32[]{:S(2)}) copy-start(bf16[2,512,512]{2,1,0:T(8,128)(2,1)} %constant.2.clone.k_hbm) | copy-start | bytes 3145732
  1.9 0.9 copy-start.2
  2.8 1.0 %copy-start.4 = (bf16[2,8,32,512]{3,2,1,0:T(8,128)(2,1)S(1)}, bf16[2,8,32,512]{3,2,1,0:T(8,128)(2,1)}, u32[]{:S(2)}) copy-start(bf16[2,8,32,512]{3,2,1,0:T(8,128)(2,1)} %probe_hbm.1) | copy-start | bytes 1572868
  3.8 0.8 copy-start.6
  4.7 0.7 copy-start.7
  5.3 60.7 %copy-start.1 = (f32[4,2,40,640]{3,2,1,0:T(8,128)S(1)}, f32[4,2,40,640]{3,2,1,0:T(8,128)}, u32[]{:S(2)}) copy-start(f32[4,2,40,640]{3,2,1,0:T(8,128)} %steps_ref.1) | copy-start | bytes 2457604
  5.3 60.7 %copy-start.3 = (f32[3,2,40,640]{3,2,1,0:T(8,128)S(1)}, f32[3,2,40,640]{3,2,1,0:T(8,128)}, u32[]{:S(2)}) copy-start(f32[3,2,40,640]{3,2,1,0:T(8,128)} %changes_ref.1) | copy-start | bytes 1843204
  5.3 60.7 %copy-start.5 = (f32[2,40,640]{2,1,0:T(8,128)S(1)}, f32[2,40,640]{2,1,0:T(8,128)}, u32[]{:S(2)}) copy-start(f32[2,40,640]{2,1,0:T(8,128)} %old_ref.1) | copy-start | bytes 614404

commit v2 on v1

v2 whole, which is shorter than its diff:
```python
import functools

import jax
import jax.numpy as jnp
import ml_dtypes
import numpy as np
from jax import lax
from jax.experimental import pallas as pl
from jax.experimental.pallas import tpu as pltpu
from jax.sharding import PartitionSpec as P

CURVE_FLOOR = 0.25
TIKHONOV = 0.5
EPSILON = 1e-06
F32 = jnp.float32
BF16 = jnp.bfloat16
LANES = 128


def propagator(count):
    index = np.arange(count)
    phase = np.outer(index, index) % count * (2.0 * np.pi / count)
    factor = 1.0 / np.sqrt(count)
    real = (np.cos(phase) * factor).astype(np.float32).astype(ml_dtypes.bfloat16)
    imag = (-np.sin(phase) * factor).astype(np.float32).astype(ml_dtypes.bfloat16)
    table = real.astype(np.float64) + 1j * imag.astype(np.float64)
    wavenumber = (index + count // 2) % count - count // 2
    chirp = np.exp(-2j * np.pi * (wavenumber * wavenumber % (4 * count)) / (4 * count))
    folded = (table * chirp[None, :]) @ table.conj()
    return np.stack([folded.real, folded.imag]).astype(np.float32).astype(ml_dtypes.bfloat16)


def dot(left, right):
    return jnp.dot(left, right, preferred_element_type=F32)


def dot_t(left, right):
    return lax.dot_general(left, right, (((1,), (1,)), ((), ())), preferred_element_type=F32)


def iota(shape, dim):
    return lax.broadcasted_iota(jnp.int32, shape, dim)


def swap(parts):
    count = len(parts)
    width = LANES // count
    lane = iota(parts[0].shape, 1)
    step = count // 2
    while step:
        low = lane % (2 * step * width) < step * width
        out = list(parts)
        for i in range(count):
            if i & step == 0:
                a, b = parts[i], parts[i + step]
                out[i] = jnp.where(low, a, pltpu.roll(b, step * width, 1))
                out[i + step] = jnp.where(low, pltpu.roll(a, LANES - step * width, 1), b)
        parts = out
        step //= 2
    return parts


def spread_sum(x, width):
    step = LANES // 2
    while step >= width:
        x = x + pltpu.roll(x, step, 1)
        step //= 2
    return x


class Exchange:
    def __init__(self, axis, size, src, dst, send, recv):
        self.axis, self.size, self.src, self.dst, self.send, self.recv = axis, size, src, dst, send, recv
        self.me = lax.axis_index(axis)

    def copy(self, peer, slot):
        return pltpu.make_async_remote_copy(
            src_ref=self.src(peer),
            dst_ref=self.dst(slot),
            send_sem=self.send.at[peer],
            recv_sem=self.recv.at[slot],
            device_id={self.axis: peer},
            device_id_type=pl.DeviceIdType.MESH,
        )

    def each(self, act):
        def one(k, carry):
            act(lax.rem(self.me + k, self.size))
            return carry

        lax.fori_loop(1, self.size, one, 0)

    def start(self):
        self.each(lambda peer: self.copy(peer, self.me).start())

    def wait_recv(self):
        self.each(lambda peer: self.copy(peer, peer).wait_recv())

    def wait_send(self):
        self.each(lambda peer: self.copy(peer, self.me).wait_send())


def signal_all(axes):
    sem = pltpu.get_barrier_semaphore()
    for name, count in axes:
        me = lax.axis_index(name)

        def signal(k, carry, name=name, count=count, me=me):
            pl.semaphore_signal(
                sem,
                inc=1,
                device_id={name: lax.rem(me + k, count)},
                device_id_type=pl.DeviceIdType.MESH,
            )
            return carry

        lax.fori_loop(1, count, signal, 0)


def wait_all(axes):
    pl.semaphore_wait(pltpu.get_barrier_semaphore(), sum(count - 1 for _, count in axes))


def step_kernel(
    grp,
    region,
    pos,
    trans_hbm,
    meas_hbm,
    probe_hbm,
    k_hbm,
    steps_hbm,
    changes_hbm,
    old_hbm,
    data_ref,
    direction_ref,
    trans,
    meas,
    probe,
    kmat,
    steps,
    changes,
    old,
    x_send,
    x_recv,
    m_send,
    m_recv,
    f_send,
    f_recv,
    b_send,
    b_recv,
    g_send,
    g_recv,
    one_send,
    one_recv,
    two_recv,
    select,
    wave,
    target,
    back_r,
    back_i,
    tile,
    gram,
    gradient,
    change,
    load_sem,
    send_sem,
    recv_sem,
    two_send_sem,
    two_recv_sem,
):
    me, here = lax.axis_index("grp"), lax.axis_index("region")
    axes = (("grp", grp), ("region", region))
    cols, length = trans.shape[1], trans.shape[2]
    modes, rows, n = probe.shape[1], probe.shape[2], probe.shape[3]
    tiles = n // LANES
    parts = 2
    width = n // (grp * parts)
    per_part = tiles // parts
    part = n // parts
    depth = steps.shape[0]
    last = depth - 1
    signal_all(axes)
    loads = [
        pltpu.make_async_copy(src, dst, load_sem.at[i])
        for i, (src, dst) in enumerate(
            (
                (trans_hbm, trans),
                (meas_hbm, meas),
                (probe_hbm, probe),
                (k_hbm, kmat),
                (steps_hbm, steps),
                (changes_hbm, changes),
                (old_hbm, old),
            )
        )
    ]
    for load in loads:
        load.start()
    row0, col0 = pos[0, 0], pos[0, 1]
    mine = pl.ds(pl.multiple_of(me * rows, rows), rows)
    phase = [0]
    copies = []

    def exchange(src, dst):
        at = phase[0]
        phase[0] += 1
        copies.append(Exchange("grp", grp, src, dst, send_sem.at[at], recv_sem.at[at]))
        return copies[-1]

    loads[0].wait()
    gap = jnp.zeros((LANES // 2 - cols, length), F32)
    block = jnp.concatenate([trans[0], gap, trans[1], gap], axis=0).astype(BF16)
    pick = iota((n, length), 1) == iota((n, length), 0) + row0
    x_send[...] = dot_t(pick.astype(F32).astype(BF16), block).astype(BF16)
    x_recv[me] = x_send[mine, :]
    wait_all(axes)
    x_copy = exchange(
        lambda p: x_send.at[pl.ds(pl.multiple_of(p * rows, rows), rows), :], lambda s: x_recv.at[s]
    )
    x_copy.start()

    loads[1].wait()
    for t in range(per_part):
        packed = swap(
            [
                meas[0, 8 * a : 8 * a + 8, LANES * (per_part * h + t) : LANES * (per_part * h + t + 1)]
                for h in range(parts)
                for a in range(rows // 8)
            ]
        )
        for g in range(8):
            m_send[8 * t + g] = packed[g]
    m_recv[me] = m_send[me]
    m_copy = exchange(lambda p: m_send.at[p], lambda s: m_recv.at[s])
    m_copy.start()

    for d in range(grp):
        lane = iota((n, LANES), 1) % (LANES // 2)
        hit = (lane + cols * d == iota((n, LANES), 0) + col0) & (lane < cols)
        select[:, LANES * d : LANES * (d + 1)] = hit.astype(F32).astype(BF16)
    loads[2].wait()
    loads[3].wait()
    x_copy.wait_recv()
    first = iota((rows, LANES), 1) < LANES // 2
    stacked = []
    for d in range(grp):
        x = x_recv[d].astype(F32)
        zero = jnp.zeros_like(x)
        stacked.append(
            jnp.concatenate([jnp.where(first, x, zero), jnp.where(first, zero, x), zero, zero], axis=0).astype(BF16)
        )
    window = jnp.transpose(dot_t(select[...], jnp.concatenate(stacked, axis=1)))
    win_r, win_i = window[:rows], window[rows : 2 * rows]
    for m in range(modes):
        p_r, p_i = probe[0, m].astype(F32), probe[1, m].astype(F32)
        wave[0, rows * m : rows * (m + 1)] = (p_r * win_r - p_i * win_i).astype(BF16)
        wave[1, rows * m : rows * (m + 1)] = (p_r * win_i + p_i * win_r).astype(BF16)

    f_copies, b_copies = [], []
    for q in range(parts):
        span = slice(part * q, part * (q + 1))
        k_r, k_i = kmat[0, :, span], kmat[1, :, span]
        out = (
            dot(wave[0], k_r) - dot(wave[1], k_i),
            dot(wave[0], k_i) + dot(wave[1], k_r),
        )
        for c in range(2):
            for t in range(per_part):
                packed = swap(
                    [out[c][rows * m : rows * (m + 1), LANES * t : LANES * (t + 1)] for m in range(modes)]
                )
                for g in range(8):
                    f_send[q, 8 * t + g, :, LANES * c : LANES * (c + 1)] = packed[g].astype(BF16)
        f_recv[q, me] = f_send[q, me]
        f_copies.append(exchange(lambda p, q=q: f_send.at[q, p], lambda s, q=q: f_recv.at[q, s]))
        f_copies[q].start()

    m_copy.wait_recv()
    packed = m_recv[...].reshape(grp * 8, LANES)
    group = iota((grp * 8, LANES), 1) // width
    for h in range(parts):
        for a in range(rows // 8):
            hit = group == h * (rows // 8) + a
            spread = spread_sum(jnp.where(hit, packed, jnp.zeros_like(packed)), width)
            target[h, :, a] = spread.reshape(grp, 8, LANES)

    for load in loads[4:]:
        load.wait()
    spots = [
        (c, slice(8 * j, 8 * j + 8), slice(LANES * t, LANES * (t + 1)))
        for c in range(2)
        for j in range(cols // 8)
        for t in range(length // LANES)
    ]
    early, late = [], []
    for i in range(depth):
        early.append(("ss", i, i))
        late += [("sg", i, i), ("yg", i, i), ("sy", i, last), ("yy", i, last)]
        for j in range(i, last):
            early += [("sy", i, j), ("yy", i, j)]
    number = {name: at for at, name in enumerate(early + late)}

    def accumulate(names, vectors):
        sums = [None] * len(names)
        for at in spots:
            value = vectors(at)
            for e, (kind, a, b) in enumerate(names):
                left = value[kind[0]][a]
                right = value["g"] if kind[1] == "g" else value[kind[1]][b]
                sums[e] = left * right if sums[e] is None else sums[e] + left * right
        for name, total in zip(names, sums):
            gram[number[name] : number[name] + 1, :] = jnp.sum(total, axis=0, keepdims=True)

    def known(at):
        return {
            "s": [steps[(i, *at)] for i in range(depth)],
            "y": [changes[(i, *at)] for i in range(last)],
        }

    accumulate(early, known)

    for q in range(parts):
        f_copies[q].wait_recv()
        x = f_recv[q].reshape(n, 2 * LANES)
        by_r, by_i = dot(kmat[0], x), dot(kmat[1], x)
        d_r = (by_r[:, :LANES] - by_i[:, LANES:]).astype(BF16).astype(F32)
        d_i = (by_r[:, LANES:] + by_i[:, :LANES]).astype(BF16).astype(F32)
        misfit = spread_sum(d_r * d_r + d_i * d_i, width) - target[q].reshape(n, LANES)
        e = jnp.concatenate([(misfit * d_r).astype(BF16), (misfit * d_i).astype(BF16)], axis=1)
        by_r, by_i = dot(kmat[0], e), dot(kmat[1], e)
        b_send[q, :, :, :LANES] = (by_r[:, :LANES] + by_i[:, LANES:]).astype(BF16).reshape(grp, rows, LANES)
        b_send[q, :, :, LANES:] = (by_r[:, LANES:] - by_i[:, :LANES]).astype(BF16).reshape(grp, rows, LANES)
        b_recv[q, me] = b_send[q, me]
        b_copies.append(exchange(lambda p, q=q: b_send.at[q, p], lambda s, q=q: b_recv.at[q, s]))
        b_copies[q].start()

    for q in range(parts):
        b_copies[q].wait_recv()
        back = []
        for c in range(2):
            by_tile = []
            for t in range(per_part):
                packed = swap(
                    [b_recv[q, 8 * t + g, :, LANES * c : LANES * (c + 1)].astype(F32) for g in range(8)]
                )
                by_tile.append(jnp.concatenate(packed, axis=0))
            back.append(jnp.concatenate(by_tile, axis=1).astype(BF16))
        span = slice(part * q, part * (q + 1))
        k_r, k_i = kmat[0, span, :], kmat[1, span, :]
        p_r = dot(back[0], k_r) + dot(back[1], k_i)
        p_i = dot(back[1], k_r) - dot(back[0], k_i)
        if q == 0:
            back_r[...] = p_r
            back_i[...] = p_i
        else:
            back_r[...] += p_r
            back_i[...] += p_i
    grad_r = jnp.zeros((rows, n), F32)
    grad_i = jnp.zeros((rows, n), F32)
    for m in range(modes):
        w_r, w_i = probe[0, m].astype(F32), probe[1, m].astype(F32)
        o_r, o_i = back_r[rows * m : rows * (m + 1)], back_i[rows * m : rows * (m + 1)]
        grad_r = grad_r + (w_r * o_r + w_i * o_i)
        grad_i = grad_i + (w_r * o_i - w_i * o_r)

    grad_r = (4.0 * grad_r).astype(BF16)
    grad_i = (4.0 * grad_i).astype(BF16)
    place = iota((length, n), 0) == iota((length, n), 1) + col0
    tall = dot_t(
        place.astype(F32).astype(BF16), jnp.concatenate([grad_r] * 4 + [grad_i] * 4, axis=0)
    )
    tall = tall.reshape(grp, cols // 8, 8, 2 * LANES)
    pieces = [
        tall[:, j, :, LANES * c : LANES * (c + 1)] for c in range(2) for j in range(cols // 8)
    ]
    group = iota((grp, 8, LANES), 2) // 32
    zero = jnp.zeros((grp, 8, LANES), F32)
    wide = []
    for w in range(4):
        value = zero
        for p in range(4):
            if 4 * w + p < len(pieces):
                value = jnp.where(group == p, pieces[4 * w + p], value)
        wide.append(value)
    g_send[...] = jnp.concatenate(wide, axis=1).astype(BF16)
    g_recv[me] = g_send[me]
    g_copy = exchange(lambda p: g_send.at[p], lambda s: g_recv.at[s])
    g_copy.start()
    put = (iota((n, length), 1) == iota((n, length), 0) + row0).astype(F32).astype(BF16)
    g_copy.wait_recv()
    for t in range(tiles):
        whole = [g_recv[4 * t + g].astype(F32) for g in range(4)]
        for w in range((len(pieces) + 3) // 4):
            packed = swap([x[8 * w : 8 * w + 8] for x in whole])
            for p in range(4):
                if 4 * w + p < len(pieces):
                    at = 8 * (4 * w + p)
                    tile[at : at + 8, LANES * t : LANES * (t + 1)] = packed[p]
    out = dot(tile[...].astype(BF16), put)
    data_ref[0] = out[:cols]
    data_ref[1] = out[cols:]

    def fresh(at):
        grad = data_ref[at] + TIKHONOV * trans[at]
        new = grad - old[at]
        gradient[at] = grad
        change[at] = new
        value = known(at)
        value["y"].append(new)
        value["g"] = grad
        return value

    accumulate(late, fresh)
    totals = jnp.sum(gram[...], axis=1, keepdims=True)
    count = gram.shape[0]
    totals = jnp.where(
        iota((count, LANES), 0) == iota((count, LANES), 1), totals, jnp.zeros((count, LANES), F32)
    )
    value = jnp.sum(totals, axis=0, keepdims=True)
    one_send[0] = value
    one_recv[me] = value
    one = exchange(lambda p: one_send.at[0], lambda s: one_recv.at[s])
    one.start()
    one.wait_recv()
    value = jnp.sum(one_recv[...], axis=0)
    one_send[1] = value
    two_recv[here] = value
    two = Exchange(
        "region", region, lambda p: one_send.at[1], lambda s: two_recv.at[s], two_send_sem, two_recv_sem
    )
    two.start()
    two.wait_recv()
    value = jnp.sum(two_recv[...], axis=0)

    def inner(kind, a, b):
        at = number[(kind, a, b)]
        return value[:, at : at + 1]

    curve = [
        jnp.maximum(inner("sy", i, i), CURVE_FLOOR * inner("ss", i, i)) for i in range(depth)
    ]
    alphas = [None] * depth
    for i in reversed(range(depth)):
        along = inner("sg", i, i)
        for j in range(i + 1, depth):
            along = along - alphas[j] * inner("sy", i, j)
        alphas[i] = along / curve[i]
    scale = curve[last] / (inner("yy", last, last) + EPSILON)
    weights = []
    for i in range(depth):
        along = inner("yg", i, i)
        for j in range(depth):
            along = along - alphas[j] * inner("yy", min(i, j), max(i, j))
        along = scale * along
        for j in range(i):
            along = along + weights[j] * inner("sy", j, i)
        weights.append(alphas[i] - along / curve[i])
    wide = lambda x: jnp.broadcast_to(x, (8, LANES))
    alphas = [wide(scale * alpha) for alpha in alphas]
    weights = [wide(weight) for weight in weights]
    scale = wide(scale)
    for at in spots:
        direction = scale * gradient[at]
        for i in range(depth):
            y = change[at] if i == last else changes[(i, *at)]
            direction = direction - alphas[i] * y + weights[i] * steps[(i, *at)]
        direction_ref[at] = direction
    for copy in (*copies, two):
        copy.wait_send()


def shards(grp, region, transmission, probe, measured, positions, past_steps, past_changes, old_gradient):
    two, cols, length = transmission.shape
    _, modes, rows, n = probe.shape
    parts = 2
    phases = 4 + 2 * parts
    vmem = pl.BlockSpec(memory_space=pltpu.VMEM)
    hbm = pl.BlockSpec(memory_space=pltpu.HBM)
    shape = jax.ShapeDtypeStruct((two, cols, length), F32)
    block = (parts, grp, rows, 2 * LANES)
    data, direction = pl.pallas_call(
        functools.partial(step_kernel, grp, region),
        out_shape=(shape, shape),
        in_specs=[pl.BlockSpec(memory_space=pltpu.SMEM)] + [hbm] * 7,
        out_specs=(vmem, vmem),
        scratch_shapes=[
            pltpu.VMEM((two, cols, length), F32),
            pltpu.VMEM(measured.shape, F32),
            pltpu.VMEM(probe.shape, BF16),
            pltpu.VMEM((2, n, n), BF16),
            pltpu.VMEM(past_steps.shape, F32),
            pltpu.VMEM(past_changes.shape, F32),
            pltpu.VMEM((two, cols, length), F32),
            pltpu.VMEM((n, LANES), BF16),
            pltpu.VMEM((grp, rows, LANES), BF16),
            pltpu.VMEM((grp, 8, LANES), F32),
            pltpu.VMEM((grp, 8, LANES), F32),
            pltpu.VMEM(block, BF16),
            pltpu.VMEM(block, BF16),
            pltpu.VMEM(block, BF16),
            pltpu.VMEM(block, BF16),
            pltpu.VMEM((grp, 32, LANES), BF16),
            pltpu.VMEM((grp, 32, LANES), BF16),
            pltpu.VMEM((2, 1, LANES), F32),
            pltpu.VMEM((grp, 1, LANES), F32),
            pltpu.VMEM((region, 1, LANES), F32),
            pltpu.VMEM((n, grp * LANES), BF16),
            pltpu.VMEM((2, modes * rows, n), BF16),
            pltpu.VMEM((parts, grp, rows // 8, 8, LANES), F32),
            pltpu.VMEM((modes * rows, n), F32),
            pltpu.VMEM((modes * rows, n), F32),
            pltpu.VMEM((two * cols, n), F32),
            pltpu.VMEM((32, LANES), F32),
            pltpu.VMEM((two, cols, length), F32),
            pltpu.VMEM((two, cols, length), F32),
            pltpu.SemaphoreType.DMA((7,)),
            pltpu.SemaphoreType.DMA((phases, grp)),
            pltpu.SemaphoreType.DMA((phases, grp)),
            pltpu.SemaphoreType.DMA((region,)),
            pltpu.SemaphoreType.DMA((region,)),
        ],
        compiler_params=pltpu.CompilerParams(
            collective_id=0, has_side_effects=True, vmem_limit_bytes=58 << 20
        ),
        name="step",
    )(
        positions,
        transmission,
        measured,
        probe,
        jnp.asarray(propagator(n)),
        past_steps,
        past_changes,
        old_gradient,
    )
    return transmission - direction, data + TIKHONOV * transmission


def solution(mesh):
    return jax.shard_map(
        functools.partial(shards, mesh.shape["grp"], mesh.shape["region"]),
        mesh=mesh,
        in_specs=(
            P(None, "grp", "region"),
            P(None, None, "grp", None),
            P("region", "grp", None),
            P("region", None),
            P(None, None, "grp", "region"),
            P(None, None, "grp", "region"),
            P(None, "grp", "region"),
        ),
        out_specs=(P(None, "grp", "region"), P(None, "grp", "region")),
        check_vma=False,
    )
```

time: 95 us -> 81.4 us (0.86)
  Pallas kernels: 87.9 us -> 78.7 us
  local copies, waits for them, and re-layouts: 6.06 us -> 0.01 us
  other arithmetic: 0 us -> 1.81 us
    pallas_call x2 -> x1, Pallas kernels: 87.9 us -> 78.7 us  [shards(): pl.pallas_call(functools.partial(step_kernel, grp, region), out_shape=(sh...]
    unnamed x18 -> x2, local copies, waits for them, and re-layouts: 6.06 us -> 0.01 us
    add x0 -> x1, other arithmetic: none -> 1.81 us  [shards(): return (transmission - direction, data + TIKHONOV * transmission)]
where the time goes in v2:
time: 81.4 us; the launch traced here: 81.2 us
  Pallas kernels  78.7 us (97%)
  other arithmetic  1.81 us (2%)
    pallas_call x1, Pallas kernels, shards(): pl.pallas_call(functools.partial(step_kernel, grp, region), out_shape=(sh...  78.7 us
    add x1, other arithmetic, shards(): return (transmission - direction, data + TIKHONOV * transmission)  1.81 us

profile of v2, /device:TPU:1, one launch (start us, length us, event | category | flops | bytes accessed | tf_op | source)
XLA Modules:
  0.0 81.2 jit_solution(1491535348292028128)
XLA Ops:
  0.6 0.0 copy-start
  0.6 78.7 %step.1 = (f32[2,40,640]{2,1,0:T(8,128)}, f32[2,40,640]{2,1,0:T(8,128)}) custom-call(s32[1,2]{1,0:T(1,128)} %pos.1, f32[2,40,640]{2,1,0:T(8,128)} %trans_hbm.1, f32[1,32,512]{2,1,0:T(8,128)} %meas_hbm.1, bf16[2,8,32,512]{3,2,1,0:T(8,128)(2,1)} %probe_hbm.1, bf16[2,512,512]{2,1,0:T(8,128)(2,1)} %constant.4.clone.k_hbm, f32[4,2,40,640]{3,2,1,0:T(8,128)} %steps_hbm.1, ...), custom_call_target="tpu_custom_call" | custom-call | tf_op jit(solution)/shard_map/step/pallas_call | solution.py:482
  79.4 0.0 copy-done
  79.4 1.8 %multiply_add_fusion = (f32[2,40,640]{2,1,0:T(8,128)}, f32[2,40,640]{2,1,0:T(8,128)}) fusion(f32[2,40,640]{2,1,0:T(8,128)} %get-tuple-element.5, f32[2,40,640]{2,1,0:T(8,128)S(1)} %copy-done, f32[2,40,640]{2,1,0:T(8,128)} %get-tuple-element.4), kind=kLoop, calls=%fused_computation | loop fusion | flops 153600 | bytes 1024000 | tf_op jit(solution)/shard_map/add | solution.py:537
Async XLA Ops:
  0.6 78.8 %copy-start = (f32[2,40,640]{2,1,0:T(8,128)S(1)}, f32[2,40,640]{2,1,0:T(8,128)}, u32[]{:S(2)}) copy-start(f32[2,40,640]{2,1,0:T(8,128)} %trans_hbm.1) | copy-start | bytes 614404

commit v3 on v2

--- a/solution.py
+++ b/solution.py
@@ -1,4 +1,5 @@
 import functools
+import itertools
 
 import jax
 import jax.numpy as jnp
@@ -68,9 +69,40 @@
     return x
 
 
+LAYOUT = {"grp": ((8, 1), (2, 2)), "region": ((8, 1), (2, 1), (2, 0.25))}
+
+
+def hops(axis, offset):
+    return sum(min(o, size - o) * far for o, (size, far) in zip(offset, LAYOUT[axis]))
+
+
+ORDER = {
+    axis: sorted(
+        (offset for offset in itertools.product(*(range(size) for size, _ in layout)) if any(offset)),
+        key=lambda offset, axis=axis: -hops(axis, offset),
+    )
+    for axis, layout in LAYOUT.items()
+}
+
+
+def peers(axis):
+    me = lax.axis_index(axis)
+    digits, unit = [], 1
+    for size, _ in reversed(LAYOUT[axis]):
+        digits.insert(0, lax.rem(lax.div(me, unit), size))
+        unit *= size
+    found = []
+    for offset in ORDER[axis]:
+        peer = 0
+        for o, digit, (size, _) in zip(offset, digits, LAYOUT[axis]):
+            peer = peer * size + (lax.rem(digit + o, size) if o else digit)
+        found.append(peer)
+    return found
+
+
 class Exchange:
-    def __init__(self, axis, size, src, dst, send, recv):
-        self.axis, self.size, self.src, self.dst, self.send, self.recv = axis, size, src, dst, send, recv
+    def __init__(self, axis, others, src, dst, send, recv):
+        self.axis, self.others, self.src, self.dst, self.send, self.recv = axis, others, src, dst, send, recv
         self.me = lax.axis_index(axis)
 
     def copy(self, peer, slot):
@@ -84,11 +116,8 @@
         )
 
     def each(self, act):
-        def one(k, carry):
-            act(lax.rem(self.me + k, self.size))
-            return carry
-
-        lax.fori_loop(1, self.size, one, 0)
+        for peer in self.others:
+            act(peer)
 
     def start(self):
         self.each(lambda peer: self.copy(peer, self.me).start())
@@ -100,25 +129,21 @@
         self.each(lambda peer: self.copy(peer, self.me).wait_send())
 
 
-def signal_all(axes):
+def signal_all(others):
     sem = pltpu.get_barrier_semaphore()
-    for name, count in axes:
-        me = lax.axis_index(name)
-
-        def signal(k, carry, name=name, count=count, me=me):
-            pl.semaphore_signal(
-                sem,
-                inc=1,
-                device_id={name: lax.rem(me + k, count)},
-                device_id_type=pl.DeviceIdType.MESH,
-            )
-            return carry
-
-        lax.fori_loop(1, count, signal, 0)
-
-
-def wait_all(axes):
-    pl.semaphore_wait(pltpu.get_barrier_semaphore(), sum(count - 1 for _, count in axes))
+    order = [
+        (hops(axis, offset), axis, peer)
+        for axis, members in others.items()
+        for offset, peer in zip(ORDER[axis], members)
+    ]
+    for _, axis, peer in sorted(order, key=lambda item: -item[0]):
+        pl.semaphore_signal(
+            sem, inc=1, device_id={axis: peer}, device_id_type=pl.DeviceIdType.MESH
+        )
+
+
+def wait_all(others):
+    pl.semaphore_wait(pltpu.get_barrier_semaphore(), sum(map(len, others.values())))
 
 
 def step_kernel(
@@ -143,8 +168,6 @@
     old,
     x_send,
     x_recv,
-    m_send,
-    m_recv,
     f_send,
     f_recv,
     b_send,
@@ -155,6 +178,7 @@
     one_recv,
     two_recv,
     select,
+    put,
     wave,
     target,
     back_r,
@@ -170,7 +194,6 @@
     two_recv_sem,
 ):
     me, here = lax.axis_index("grp"), lax.axis_index("region")
-    axes = (("grp", grp), ("region", region))
     cols, length = trans.shape[1], trans.shape[2]
     modes, rows, n = probe.shape[1], probe.shape[2], probe.shape[3]
     tiles = n // LANES
@@ -180,7 +203,8 @@
     part = n // parts
     depth = steps.shape[0]
     last = depth - 1
-    signal_all(axes)
+    groups = LANES // width
+    slots = (groups // 2 - 1, groups - 1)
     loads = [
         pltpu.make_async_copy(src, dst, load_sem.at[i])
         for i, (src, dst) in enumerate(
@@ -195,45 +219,42 @@
             )
         )
     ]
-    for load in loads:
+    for load in loads[:2]:
         load.start()
+    others = {axis: peers(axis) for axis in ("grp", "region")}
+    signal_all(others)
     row0, col0 = pos[0, 0], pos[0, 1]
-    mine = pl.ds(pl.multiple_of(me * rows, rows), rows)
     phase = [0]
     copies = []
 
     def exchange(src, dst):
         at = phase[0]
         phase[0] += 1
-        copies.append(Exchange("grp", grp, src, dst, send_sem.at[at], recv_sem.at[at]))
+        copies.append(Exchange("grp", others["grp"], src, dst, send_sem.at[at], recv_sem.at[at]))
         return copies[-1]
 
-    loads[0].wait()
+    pick = iota((n, length), 1) == iota((n, length), 0) + row0
+    put[...] = pick.astype(F32).astype(BF16)
+    group = iota((rows, LANES), 1) // width
+    for load in loads[:2]:
+        load.wait()
+    for load in loads[2:]:
+        load.start()
     gap = jnp.zeros((LANES // 2 - cols, length), F32)
     block = jnp.concatenate([trans[0], gap, trans[1], gap], axis=0).astype(BF16)
-    pick = iota((n, length), 1) == iota((n, length), 0) + row0
-    x_send[...] = dot_t(pick.astype(F32).astype(BF16), block).astype(BF16)
-    x_recv[me] = x_send[mine, :]
-    wait_all(axes)
-    x_copy = exchange(
-        lambda p: x_send.at[pl.ds(pl.multiple_of(p * rows, rows), rows), :], lambda s: x_recv.at[s]
-    )
+    seen = dot_t(put[...], block)
+    for d in range(grp):
+        value = seen[rows * d : rows * (d + 1)]
+        for h, at in enumerate(slots):
+            t, g = per_part * h + d // groups, d % groups
+            moved = pltpu.roll(meas[0, :, LANES * t : LANES * (t + 1)], (width * (at - g)) % LANES, 1)
+            value = jnp.where(group == at, moved, value)
+        x_send[d] = value.astype(BF16)
+    x_recv[me] = x_send[me]
+
+    wait_all(others)
+    x_copy = exchange(lambda p: x_send.at[p], lambda s: x_recv.at[s])
     x_copy.start()
-
-    loads[1].wait()
-    for t in range(per_part):
-        packed = swap(
-            [
-                meas[0, 8 * a : 8 * a + 8, LANES * (per_part * h + t) : LANES * (per_part * h + t + 1)]
-                for h in range(parts)
-                for a in range(rows // 8)
-            ]
-        )
-        for g in range(8):
-            m_send[8 * t + g] = packed[g]
-    m_recv[me] = m_send[me]
-    m_copy = exchange(lambda p: m_send.at[p], lambda s: m_recv.at[s])
-    m_copy.start()
 
     for d in range(grp):
         lane = iota((n, LANES), 1) % (LANES // 2)
@@ -276,14 +297,10 @@
         f_copies.append(exchange(lambda p, q=q: f_send.at[q, p], lambda s, q=q: f_recv.at[q, s]))
         f_copies[q].start()
 
-    m_copy.wait_recv()
-    packed = m_recv[...].reshape(grp * 8, LANES)
-    group = iota((grp * 8, LANES), 1) // width
-    for h in range(parts):
-        for a in range(rows // 8):
-            hit = group == h * (rows // 8) + a
-            spread = spread_sum(jnp.where(hit, packed, jnp.zeros_like(packed)), width)
-            target[h, :, a] = spread.reshape(grp, 8, LANES)
+    seen = x_recv[...].astype(F32).reshape(n, LANES)
+    group = iota((n, LANES), 1) // width
+    for h, at in enumerate(slots):
+        target[h] = spread_sum(jnp.where(group == at, seen, jnp.zeros_like(seen)), width)
 
     for load in loads[4:]:
         load.wait()
@@ -326,7 +343,7 @@
         by_r, by_i = dot(kmat[0], x), dot(kmat[1], x)
         d_r = (by_r[:, :LANES] - by_i[:, LANES:]).astype(BF16).astype(F32)
         d_i = (by_r[:, LANES:] + by_i[:, :LANES]).astype(BF16).astype(F32)
-        misfit = spread_sum(d_r * d_r + d_i * d_i, width) - target[q].reshape(n, LANES)
+        misfit = spread_sum(d_r * d_r + d_i * d_i, width) - target[q]
         e = jnp.concatenate([(misfit * d_r).astype(BF16), (misfit * d_i).astype(BF16)], axis=1)
         by_r, by_i = dot(kmat[0], e), dot(kmat[1], e)
         b_send[q, :, :, :LANES] = (by_r[:, :LANES] + by_i[:, LANES:]).astype(BF16).reshape(grp, rows, LANES)
@@ -387,7 +404,6 @@
     g_recv[me] = g_send[me]
     g_copy = exchange(lambda p: g_send.at[p], lambda s: g_recv.at[s])
     g_copy.start()
-    put = (iota((n, length), 1) == iota((n, length), 0) + row0).astype(F32).astype(BF16)
     g_copy.wait_recv()
     for t in range(tiles):
         whole = [g_recv[4 * t + g].astype(F32) for g in range(4)]
@@ -397,7 +413,7 @@
                 if 4 * w + p < len(pieces):
                     at = 8 * (4 * w + p)
                     tile[at : at + 8, LANES * t : LANES * (t + 1)] = packed[p]
-    out = dot(tile[...].astype(BF16), put)
+    out = dot(tile[...].astype(BF16), put[...])
     data_ref[0] = out[:cols]
     data_ref[1] = out[cols:]
 
@@ -427,7 +443,12 @@
     one_send[1] = value
     two_recv[here] = value
     two = Exchange(
-        "region", region, lambda p: one_send.at[1], lambda s: two_recv.at[s], two_send_sem, two_recv_sem
+        "region",
+        others["region"],
+        lambda p: one_send.at[1],
+        lambda s: two_recv.at[s],
+        two_send_sem,
+        two_recv_sem,
     )
     two.start()
     two.wait_recv()
@@ -474,7 +495,7 @@
     two, cols, length = transmission.shape
     _, modes, rows, n = probe.shape
     parts = 2
-    phases = 4 + 2 * parts
+    phases = 3 + 2 * parts
     vmem = pl.BlockSpec(memory_space=pltpu.VMEM)
     hbm = pl.BlockSpec(memory_space=pltpu.HBM)
     shape = jax.ShapeDtypeStruct((two, cols, length), F32)
@@ -492,10 +513,8 @@
             pltpu.VMEM(past_steps.shape, F32),
             pltpu.VMEM(past_changes.shape, F32),
             pltpu.VMEM((two, cols, length), F32),
-            pltpu.VMEM((n, LANES), BF16),
             pltpu.VMEM((grp, rows, LANES), BF16),
-            pltpu.VMEM((grp, 8, LANES), F32),
-            pltpu.VMEM((grp, 8, LANES), F32),
+            pltpu.VMEM((grp, rows, LANES), BF16),
             pltpu.VMEM(block, BF16),
             pltpu.VMEM(block, BF16),
             pltpu.VMEM(block, BF16),
@@ -506,8 +525,9 @@
             pltpu.VMEM((grp, 1, LANES), F32),
             pltpu.VMEM((region, 1, LANES), F32),
             pltpu.VMEM((n, grp * LANES), BF16),
+            pltpu.VMEM((n, length), BF16),
             pltpu.VMEM((2, modes * rows, n), BF16),
-            pltpu.VMEM((parts, grp, rows // 8, 8, LANES), F32),
+            pltpu.VMEM((parts, n, LANES), F32),
             pltpu.VMEM((modes * rows, n), F32),
             pltpu.VMEM((modes * rows, n), F32),
             pltpu.VMEM((two * cols, n), F32),

time: 81.4 us -> 75.5 us (0.928)
  Pallas kernels: 78.7 us -> 72.8 us
    pallas_call x1, Pallas kernels: 78.7 us -> 72.8 us  [shards(): pl.pallas_call(functools.partial(step_kernel, grp, region), out_shape=(sh...]
where the time goes in v3:
time: 75.5 us; the launch traced here: 75.3 us
  Pallas kernels  72.8 us (96%)
  other arithmetic  1.81 us (2%)
    pallas_call x1, Pallas kernels, shards(): pl.pallas_call(functools.partial(step_kernel, grp, region), out_shape=(sh...  72.8 us
    add x1, other arithmetic, shards(): return (transmission - direction, data + TIKHONOV * transmission)  1.81 us

profile of v3, /device:TPU:1, one launch (start us, length us, event | category | flops | bytes accessed | tf_op | source)
XLA Modules:
  0.0 75.3 jit_solution(4126664557539268294)
XLA Ops:
  0.6 0.0 copy-start
  0.6 72.8 %step.1 = (f32[2,40,640]{2,1,0:T(8,128)}, f32[2,40,640]{2,1,0:T(8,128)}) custom-call(s32[1,2]{1,0:T(1,128)} %pos.1, f32[2,40,640]{2,1,0:T(8,128)} %trans_hbm.1, f32[1,32,512]{2,1,0:T(8,128)} %meas_hbm.1, bf16[2,8,32,512]{3,2,1,0:T(8,128)(2,1)} %probe_hbm.1, bf16[2,512,512]{2,1,0:T(8,128)(2,1)} %constant.4.clone.k_hbm, f32[4,2,40,640]{3,2,1,0:T(8,128)} %steps_hbm.1, ...), custom_call_target="tpu_custom_call" | custom-call | tf_op jit(solution)/shard_map/step/pallas_call | solution.py:503
  73.5 0.0 copy-done
  73.5 1.8 %multiply_add_fusion = (f32[2,40,640]{2,1,0:T(8,128)}, f32[2,40,640]{2,1,0:T(8,128)}) fusion(f32[2,40,640]{2,1,0:T(8,128)} %get-tuple-element.5, f32[2,40,640]{2,1,0:T(8,128)S(1)} %copy-done, f32[2,40,640]{2,1,0:T(8,128)} %get-tuple-element.4), kind=kLoop, calls=%fused_computation | loop fusion | flops 153600 | bytes 1024000 | tf_op jit(solution)/shard_map/add | solution.py:557
Async XLA Ops:
  0.6 72.9 %copy-start = (f32[2,40,640]{2,1,0:T(8,128)S(1)}, f32[2,40,640]{2,1,0:T(8,128)}, u32[]{:S(2)}) copy-start(f32[2,40,640]{2,1,0:T(8,128)} %trans_hbm.1) | copy-start | bytes 614404

commit v4 on v3

--- a/solution.py
+++ b/solution.py
@@ -149,7 +149,7 @@
 def step_kernel(
     grp,
     region,
-    pos,
+    pos_hbm,
     trans_hbm,
     meas_hbm,
     probe_hbm,
@@ -159,6 +159,7 @@
     old_hbm,
     data_ref,
     direction_ref,
+    pos,
     trans,
     meas,
     probe,
@@ -209,6 +210,7 @@
         pltpu.make_async_copy(src, dst, load_sem.at[i])
         for i, (src, dst) in enumerate(
             (
+                (pos_hbm, pos),
                 (trans_hbm, trans),
                 (meas_hbm, meas),
                 (probe_hbm, probe),
@@ -219,10 +221,11 @@
             )
         )
     ]
-    for load in loads[:2]:
+    for load in loads[:3]:
         load.start()
     others = {axis: peers(axis) for axis in ("grp", "region")}
     signal_all(others)
+    loads[0].wait()
     row0, col0 = pos[0, 0], pos[0, 1]
     phase = [0]
     copies = []
@@ -236,9 +239,9 @@
     pick = iota((n, length), 1) == iota((n, length), 0) + row0
     put[...] = pick.astype(F32).astype(BF16)
     group = iota((rows, LANES), 1) // width
-    for load in loads[:2]:
+    for load in loads[1:3]:
         load.wait()
-    for load in loads[2:]:
+    for load in loads[3:]:
         load.start()
     gap = jnp.zeros((LANES // 2 - cols, length), F32)
     block = jnp.concatenate([trans[0], gap, trans[1], gap], axis=0).astype(BF16)
@@ -260,8 +263,8 @@
         lane = iota((n, LANES), 1) % (LANES // 2)
         hit = (lane + cols * d == iota((n, LANES), 0) + col0) & (lane < cols)
         select[:, LANES * d : LANES * (d + 1)] = hit.astype(F32).astype(BF16)
-    loads[2].wait()
     loads[3].wait()
+    loads[4].wait()
     x_copy.wait_recv()
     first = iota((rows, LANES), 1) < LANES // 2
     stacked = []
@@ -302,7 +305,7 @@
     for h, at in enumerate(slots):
         target[h] = spread_sum(jnp.where(group == at, seen, jnp.zeros_like(seen)), width)
 
-    for load in loads[4:]:
+    for load in loads[5:]:
         load.wait()
     spots = [
         (c, slice(8 * j, 8 * j + 8), slice(LANES * t, LANES * (t + 1)))
@@ -481,12 +484,15 @@
     alphas = [wide(scale * alpha) for alpha in alphas]
     weights = [wide(weight) for weight in weights]
     scale = wide(scale)
-    for at in spots:
-        direction = scale * gradient[at]
-        for i in range(depth):
-            y = change[at] if i == last else changes[(i, *at)]
-            direction = direction - alphas[i] * y + weights[i] * steps[(i, *at)]
-        direction_ref[at] = direction
+    for c in range(2):
+        for at in spots:
+            if at[0] != c:
+                continue
+            direction = scale * gradient[at]
+            for i in range(depth):
+                y = change[at] if i == last else changes[(i, *at)]
+                direction = direction - alphas[i] * y + weights[i] * steps[(i, *at)]
+            direction_ref[at] = direction
     for copy in (*copies, two):
         copy.wait_send()
 
@@ -496,16 +502,16 @@
     _, modes, rows, n = probe.shape
     parts = 2
     phases = 3 + 2 * parts
-    vmem = pl.BlockSpec(memory_space=pltpu.VMEM)
     hbm = pl.BlockSpec(memory_space=pltpu.HBM)
     shape = jax.ShapeDtypeStruct((two, cols, length), F32)
     block = (parts, grp, rows, 2 * LANES)
     data, direction = pl.pallas_call(
         functools.partial(step_kernel, grp, region),
         out_shape=(shape, shape),
-        in_specs=[pl.BlockSpec(memory_space=pltpu.SMEM)] + [hbm] * 7,
-        out_specs=(vmem, vmem),
+        in_specs=[hbm] * 8,
+        out_specs=(pl.BlockSpec(memory_space=pltpu.VMEM),) * 2,
         scratch_shapes=[
+            pltpu.SMEM(positions.shape, jnp.int32),
             pltpu.VMEM((two, cols, length), F32),
             pltpu.VMEM(measured.shape, F32),
             pltpu.VMEM(probe.shape, BF16),
@@ -534,25 +540,30 @@
             pltpu.VMEM((32, LANES), F32),
             pltpu.VMEM((two, cols, length), F32),
             pltpu.VMEM((two, cols, length), F32),
-            pltpu.SemaphoreType.DMA((7,)),
+            pltpu.SemaphoreType.DMA((8,)),
             pltpu.SemaphoreType.DMA((phases, grp)),
             pltpu.SemaphoreType.DMA((phases, grp)),
             pltpu.SemaphoreType.DMA((region,)),
             pltpu.SemaphoreType.DMA((region,)),
         ],
         compiler_params=pltpu.CompilerParams(
-            collective_id=0, has_side_effects=True, vmem_limit_bytes=58 << 20
+            collective_id=0, has_side_effects=True, vmem_limit_bytes=48 << 20
         ),
         name="step",
     )(
-        positions,
-        transmission,
-        measured,
-        probe,
-        jnp.asarray(propagator(n)),
-        past_steps,
-        past_changes,
-        old_gradient,
+        *(
+            pltpu.with_memory_space_constraint(operand, pltpu.HBM)
+            for operand in (
+                positions,
+                transmission,
+                measured,
+                probe,
+                jnp.asarray(propagator(n)),
+                past_steps,
+                past_changes,
+                old_gradient,
+            )
+        )
     )
     return transmission - direction, data + TIKHONOV * transmission
 

time: 75.5 us -> 73 us (0.967)
  Pallas kernels: 72.8 us -> 71.4 us
  other arithmetic: 1.81 us -> 0.79 us
    pallas_call x1, Pallas kernels: 72.8 us -> 71.4 us  [shards(): pl.pallas_call(functools.partial(step_kernel, grp, region), out_shape=(sh...]
    add x1, other arithmetic: 1.81 us -> 0.79 us  [shards(): return (transmission - direction, data + TIKHONOV * transmission)]
where the time goes in v4:
time: 73 us; the launch traced here: 72.9 us
  Pallas kernels  71.4 us (98%)
  other arithmetic  0.79 us (1%)
    pallas_call x1, Pallas kernels, shards(): pl.pallas_call(functools.partial(step_kernel, grp, region), out_shape=(sh...  71.4 us

profile of v4, /device:TPU:1, one launch (start us, length us, event | category | flops | bytes accessed | tf_op | source)
XLA Modules:
  0.0 72.9 jit_solution(7881535523852833934)
XLA Ops:
  0.6 0.0 copy-start
  0.6 71.4 %step.1 = (f32[2,40,640]{2,1,0:T(8,128)S(1)}, f32[2,40,640]{2,1,0:T(8,128)S(1)}) custom-call(s32[1,2]{1,0:T(1,128)} %pos_hbm.1, f32[2,40,640]{2,1,0:T(8,128)} %trans_hbm.1, f32[1,32,512]{2,1,0:T(8,128)} %meas_hbm.1, bf16[2,8,32,512]{3,2,1,0:T(8,128)(2,1)} %probe_hbm.1, bf16[2,512,512]{2,1,0:T(8,128)(2,1)} %constant.4.clone.k_hbm, ...), custom_call_target="tpu_custom_call" | custom-call | tf_op jit(solution)/shard_map/step/pallas_call | solution.py:508
  72.1 0.0 copy-done
  72.1 0.8 %multiply_add_fusion = (f32[2,40,640]{2,1,0:T(8,128)}, f32[2,40,640]{2,1,0:T(8,128)}) fusion(f32[2,40,640]{2,1,0:T(8,128)S(1)} %get-tuple-element.5, f32[2,40,640]{2,1,0:T(8,128)S(1)} %copy-done, f32[2,40,640]{2,1,0:T(8,128)S(1)} %get-tuple-element.4), kind=kLoop, calls=%fused_computation | loop fusion | flops 153600 | bytes 1024000 | tf_op jit(solution)/shard_map/add | solution.py:568
Async XLA Ops:
  0.6 71.4 %copy-start = (f32[2,40,640]{2,1,0:T(8,128)S(1)}, f32[2,40,640]{2,1,0:T(8,128)}, u32[]{:S(2)}) copy-start(f32[2,40,640]{2,1,0:T(8,128)} %trans_hbm.1) | copy-start | bytes 614404

commit v5 on v4

--- a/solution.py
+++ b/solution.py
@@ -101,32 +101,41 @@
 
 
 class Exchange:
-    def __init__(self, axis, others, src, dst, send, recv):
-        self.axis, self.others, self.src, self.dst, self.send, self.recv = axis, others, src, dst, send, recv
+    def __init__(self, axis, others, src, dst, send, recv, shared=False):
+        self.axis, self.others, self.src, self.dst = axis, others, src, dst
+        self.send, self.recv, self.shared = send, recv, shared
         self.me = lax.axis_index(axis)
 
-    def copy(self, peer, slot):
+    def copy(self, src, dst):
         return pltpu.make_async_remote_copy(
-            src_ref=self.src(peer),
-            dst_ref=self.dst(slot),
-            send_sem=self.send.at[peer],
-            recv_sem=self.recv.at[slot],
-            device_id={self.axis: peer},
+            src_ref=src,
+            dst_ref=dst,
+            send_sem=self.send,
+            recv_sem=self.recv,
+            device_id={self.axis: self.others[0]},
             device_id_type=pl.DeviceIdType.MESH,
         )
 
-    def each(self, act):
+    def start(self):
         for peer in self.others:
-            act(peer)
-
-    def start(self):
-        self.each(lambda peer: self.copy(peer, self.me).start())
+            pltpu.make_async_remote_copy(
+                src_ref=self.src if self.shared else self.src.at[peer],
+                dst_ref=self.dst.at[self.me],
+                send_sem=self.send,
+                recv_sem=self.recv,
+                device_id={self.axis: peer},
+                device_id_type=pl.DeviceIdType.MESH,
+            ).start()
+
+    def bulk(self):
+        every = self.dst.at[pl.ds(0, len(self.others))]
+        return self.copy(every, every)
 
     def wait_recv(self):
-        self.each(lambda peer: self.copy(peer, peer).wait_recv())
+        self.bulk().wait_recv()
 
     def wait_send(self):
-        self.each(lambda peer: self.copy(peer, self.me).wait_send())
+        self.bulk().wait_send()
 
 
 def signal_all(others):
@@ -182,8 +191,7 @@
     put,
     wave,
     target,
-    back_r,
-    back_i,
+    shift,
     tile,
     gram,
     gradient,
@@ -191,8 +199,6 @@
     load_sem,
     send_sem,
     recv_sem,
-    two_send_sem,
-    two_recv_sem,
 ):
     me, here = lax.axis_index("grp"), lax.axis_index("region")
     cols, length = trans.shape[1], trans.shape[2]
@@ -230,10 +236,10 @@
     phase = [0]
     copies = []
 
-    def exchange(src, dst):
+    def exchange(src, dst, axis="grp", shared=False):
         at = phase[0]
         phase[0] += 1
-        copies.append(Exchange("grp", others["grp"], src, dst, send_sem.at[at], recv_sem.at[at]))
+        copies.append(Exchange(axis, others[axis], src, dst, send_sem.at[at], recv_sem.at[at], shared))
         return copies[-1]
 
     pick = iota((n, length), 1) == iota((n, length), 0) + row0
@@ -256,7 +262,7 @@
     x_recv[me] = x_send[me]
 
     wait_all(others)
-    x_copy = exchange(lambda p: x_send.at[p], lambda s: x_recv.at[s])
+    x_copy = exchange(x_send, x_recv)
     x_copy.start()
 
     for d in range(grp):
@@ -297,7 +303,7 @@
                 for g in range(8):
                     f_send[q, 8 * t + g, :, LANES * c : LANES * (c + 1)] = packed[g].astype(BF16)
         f_recv[q, me] = f_send[q, me]
-        f_copies.append(exchange(lambda p, q=q: f_send.at[q, p], lambda s, q=q: f_recv.at[q, s]))
+        f_copies.append(exchange(f_send.at[q], f_recv.at[q]))
         f_copies[q].start()
 
     seen = x_recv[...].astype(F32).reshape(n, LANES)
@@ -352,9 +358,13 @@
         b_send[q, :, :, :LANES] = (by_r[:, :LANES] + by_i[:, LANES:]).astype(BF16).reshape(grp, rows, LANES)
         b_send[q, :, :, LANES:] = (by_r[:, LANES:] - by_i[:, :LANES]).astype(BF16).reshape(grp, rows, LANES)
         b_recv[q, me] = b_send[q, me]
-        b_copies.append(exchange(lambda p, q=q: b_send.at[q, p], lambda s, q=q: b_recv.at[q, s]))
+        b_copies.append(exchange(b_send.at[q], b_recv.at[q]))
         b_copies[q].start()
 
+    place = iota((length, n), 0) == iota((length, n), 1) + col0
+    shift[...] = place.astype(F32).astype(BF16)
+    grad_r = jnp.zeros((rows, n), F32)
+    grad_i = jnp.zeros((rows, n), F32)
     for q in range(parts):
         b_copies[q].wait_recv()
         back = []
@@ -370,26 +380,15 @@
         k_r, k_i = kmat[0, span, :], kmat[1, span, :]
         p_r = dot(back[0], k_r) + dot(back[1], k_i)
         p_i = dot(back[1], k_r) - dot(back[0], k_i)
-        if q == 0:
-            back_r[...] = p_r
-            back_i[...] = p_i
-        else:
-            back_r[...] += p_r
-            back_i[...] += p_i
-    grad_r = jnp.zeros((rows, n), F32)
-    grad_i = jnp.zeros((rows, n), F32)
-    for m in range(modes):
-        w_r, w_i = probe[0, m].astype(F32), probe[1, m].astype(F32)
-        o_r, o_i = back_r[rows * m : rows * (m + 1)], back_i[rows * m : rows * (m + 1)]
-        grad_r = grad_r + (w_r * o_r + w_i * o_i)
-        grad_i = grad_i + (w_r * o_i - w_i * o_r)
+        for m in range(modes):
+            w_r, w_i = probe[0, m].astype(F32), probe[1, m].astype(F32)
+            o_r, o_i = p_r[rows * m : rows * (m + 1)], p_i[rows * m : rows * (m + 1)]
+            grad_r = grad_r + (w_r * o_r + w_i * o_i)
+            grad_i = grad_i + (w_r * o_i - w_i * o_r)
 
     grad_r = (4.0 * grad_r).astype(BF16)
     grad_i = (4.0 * grad_i).astype(BF16)
-    place = iota((length, n), 0) == iota((length, n), 1) + col0
-    tall = dot_t(
-        place.astype(F32).astype(BF16), jnp.concatenate([grad_r] * 4 + [grad_i] * 4, axis=0)
-    )
+    tall = dot_t(shift[...], jnp.concatenate([grad_r] * 4 + [grad_i] * 4, axis=0))
     tall = tall.reshape(grp, cols // 8, 8, 2 * LANES)
     pieces = [
         tall[:, j, :, LANES * c : LANES * (c + 1)] for c in range(2) for j in range(cols // 8)
@@ -405,7 +404,7 @@
         wide.append(value)
     g_send[...] = jnp.concatenate(wide, axis=1).astype(BF16)
     g_recv[me] = g_send[me]
-    g_copy = exchange(lambda p: g_send.at[p], lambda s: g_recv.at[s])
+    g_copy = exchange(g_send, g_recv)
     g_copy.start()
     g_copy.wait_recv()
     for t in range(tiles):
@@ -439,20 +438,13 @@
     value = jnp.sum(totals, axis=0, keepdims=True)
     one_send[0] = value
     one_recv[me] = value
-    one = exchange(lambda p: one_send.at[0], lambda s: one_recv.at[s])
+    one = exchange(one_send.at[0], one_recv, shared=True)
     one.start()
     one.wait_recv()
     value = jnp.sum(one_recv[...], axis=0)
     one_send[1] = value
     two_recv[here] = value
-    two = Exchange(
-        "region",
-        others["region"],
-        lambda p: one_send.at[1],
-        lambda s: two_recv.at[s],
-        two_send_sem,
-        two_recv_sem,
-    )
+    two = exchange(one_send.at[1], two_recv, "region", shared=True)
     two.start()
     two.wait_recv()
     value = jnp.sum(two_recv[...], axis=0)
@@ -493,7 +485,7 @@
                 y = change[at] if i == last else changes[(i, *at)]
                 direction = direction - alphas[i] * y + weights[i] * steps[(i, *at)]
             direction_ref[at] = direction
-    for copy in (*copies, two):
+    for copy in copies:
         copy.wait_send()
 
 
@@ -501,7 +493,7 @@
     two, cols, length = transmission.shape
     _, modes, rows, n = probe.shape
     parts = 2
-    phases = 3 + 2 * parts
+    phases = 4 + 2 * parts
     hbm = pl.BlockSpec(memory_space=pltpu.HBM)
     shape = jax.ShapeDtypeStruct((two, cols, length), F32)
     block = (parts, grp, rows, 2 * LANES)
@@ -534,17 +526,14 @@
             pltpu.VMEM((n, length), BF16),
             pltpu.VMEM((2, modes * rows, n), BF16),
             pltpu.VMEM((parts, n, LANES), F32),
-            pltpu.VMEM((modes * rows, n), F32),
-            pltpu.VMEM((modes * rows, n), F32),
+            pltpu.VMEM((length, n), BF16),
             pltpu.VMEM((two * cols, n), F32),
             pltpu.VMEM((32, LANES), F32),
             pltpu.VMEM((two, cols, length), F32),
             pltpu.VMEM((two, cols, length), F32),
             pltpu.SemaphoreType.DMA((8,)),
-            pltpu.SemaphoreType.DMA((phases, grp)),
-            pltpu.SemaphoreType.DMA((phases, grp)),
-            pltpu.SemaphoreType.DMA((region,)),
-            pltpu.SemaphoreType.DMA((region,)),
+            pltpu.SemaphoreType.DMA((phases,)),
+            pltpu.SemaphoreType.DMA((phases,)),
         ],
         compiler_params=pltpu.CompilerParams(
             collective_id=0, has_side_effects=True, vmem_limit_bytes=48 << 20

time: 73 us -> 70.2 us (0.962)
  Pallas kernels: 71.4 us -> 68.7 us
    pallas_call x1, Pallas kernels: 71.4 us -> 68.7 us  [shards(): pl.pallas_call(functools.partial(step_kernel, grp, region), out_shape=(sh...]
where the time goes in v5:
time: 70.2 us; the launch traced here: 70.1 us
  Pallas kernels  68.7 us (98%)
  other arithmetic  0.79 us (1%)
    pallas_call x1, Pallas kernels, shards(): pl.pallas_call(functools.partial(step_kernel, grp, region), out_shape=(sh...  68.7 us

profile of v5, /device:TPU:1, one launch (start us, length us, event | category | flops | bytes accessed | tf_op | source)
XLA Modules:
  0.0 70.1 jit_solution(422817099900117547)
XLA Ops:
  0.6 0.0 copy-start
  0.6 68.7 %step.1 = (f32[2,40,640]{2,1,0:T(8,128)S(1)}, f32[2,40,640]{2,1,0:T(8,128)S(1)}) custom-call(s32[1,2]{1,0:T(1,128)} %pos_hbm.1, f32[2,40,640]{2,1,0:T(8,128)} %trans_hbm.1, f32[1,32,512]{2,1,0:T(8,128)} %meas_hbm.1, bf16[2,8,32,512]{3,2,1,0:T(8,128)(2,1)} %probe_hbm.1, bf16[2,512,512]{2,1,0:T(8,128)(2,1)} %constant.4.clone.k_hbm, ...), custom_call_target="tpu_custom_call" | custom-call | tf_op jit(solution)/shard_map/step/pallas_call | solution.py:500
  69.3 0.0 copy-done
  69.3 0.8 %multiply_add_fusion = (f32[2,40,640]{2,1,0:T(8,128)}, f32[2,40,640]{2,1,0:T(8,128)}) fusion(f32[2,40,640]{2,1,0:T(8,128)S(1)} %get-tuple-element.5, f32[2,40,640]{2,1,0:T(8,128)S(1)} %copy-done, f32[2,40,640]{2,1,0:T(8,128)S(1)} %get-tuple-element.4), kind=kLoop, calls=%fused_computation | loop fusion | flops 153600 | bytes 1024000 | tf_op jit(solution)/shard_map/add | solution.py:557
Async XLA Ops:
  0.6 68.7 %copy-start = (f32[2,40,640]{2,1,0:T(8,128)S(1)}, f32[2,40,640]{2,1,0:T(8,128)}, u32[]{:S(2)}) copy-start(f32[2,40,640]{2,1,0:T(8,128)} %trans_hbm.1) | copy-start | bytes 614404

commit v6 on v5

--- a/solution.py
+++ b/solution.py
@@ -1,5 +1,6 @@
 import functools
 import itertools
+import math
 
 import jax
 import jax.numpy as jnp
@@ -69,67 +70,70 @@
     return x
 
 
-LAYOUT = {"grp": ((8, 1), (2, 2)), "region": ((8, 1), (2, 1), (2, 0.25))}
-
-
-def hops(axis, offset):
-    return sum(min(o, size - o) * far for o, (size, far) in zip(offset, LAYOUT[axis]))
-
-
-ORDER = {
-    axis: sorted(
-        (offset for offset in itertools.product(*(range(size) for size, _ in layout)) if any(offset)),
-        key=lambda offset, axis=axis: -hops(axis, offset),
-    )
-    for axis, layout in LAYOUT.items()
+PLACE = {
+    "z": ("grp", 2, 8),
+    "x_hi": ("grp", 1, 2),
+    "y": ("region", 4, 8),
+    "x_lo": ("region", 2, 2),
+    "core": ("region", 1, 2),
 }
-
-
-def peers(axis):
-    me = lax.axis_index(axis)
-    digits, unit = [], 1
-    for size, _ in reversed(LAYOUT[axis]):
-        digits.insert(0, lax.rem(lax.div(me, unit), size))
-        unit *= size
-    found = []
-    for offset in ORDER[axis]:
-        peer = 0
-        for o, digit, (size, _) in zip(offset, digits, LAYOUT[axis]):
-            peer = peer * size + (lax.rem(digit + o, size) if o else digit)
-        found.append(peer)
-    return found
+TEAMS = {"rows": ("z", "x_hi"), "plane": ("z", "x_hi", "x_lo"), "line": ("y", "core")}
+
+
+def hops(step):
+    z, y = (min(step.get(name, 0), 8 - step.get(name, 0)) for name in ("z", "y"))
+    x = 2 * step.get("x_hi", 0) + step.get("x_lo", 0)
+    return z + y + min(x, 4 - x) + 0.25 * step.get("core", 0)
+
+
+class Team:
+    def __init__(self, names, digits):
+        self.size = math.prod(PLACE[name][2] for name in names)
+        self.me = 0
+        for name in names:
+            self.me = self.me * PLACE[name][2] + digits[name]
+        steps = itertools.product(*(range(PLACE[name][2]) for name in names))
+        steps = [dict(zip(names, step)) for step in steps if any(step)]
+        self.hops, self.others = [], []
+        for step in sorted(steps, key=lambda step: -hops(step)):
+            place, number = {}, 0
+            for name in names:
+                axis, unit, size = PLACE[name]
+                digit = lax.rem(digits[name] + step[name], size) if step[name] else digits[name]
+                number = number * size + digit
+            for axis in sorted({PLACE[name][0] for name in names}):
+                place[axis] = sum(
+                    (lax.rem(digits[name] + step[name], size) if step.get(name) else digits[name]) * unit
+                    for name, (on, unit, size) in PLACE.items()
+                    if on == axis
+                )
+            self.hops.append(hops(step))
+            self.others.append((number, place))
 
 
 class Exchange:
-    def __init__(self, axis, others, src, dst, send, recv, shared=False):
-        self.axis, self.others, self.src, self.dst = axis, others, src, dst
+    def __init__(self, team, src, dst, send, recv, shared=False):
+        self.team, self.src, self.dst = team, src, dst
         self.send, self.recv, self.shared = send, recv, shared
-        self.me = lax.axis_index(axis)
-
-    def copy(self, src, dst):
+
+    def copy(self, src, dst, place):
         return pltpu.make_async_remote_copy(
             src_ref=src,
             dst_ref=dst,
             send_sem=self.send,
             recv_sem=self.recv,
-            device_id={self.axis: self.others[0]},
+            device_id=place,
             device_id_type=pl.DeviceIdType.MESH,
         )
 
     def start(self):
-        for peer in self.others:
-            pltpu.make_async_remote_copy(
-                src_ref=self.src if self.shared else self.src.at[peer],
-                dst_ref=self.dst.at[self.me],
-                send_sem=self.send,
-                recv_sem=self.recv,
-                device_id={self.axis: peer},
-                device_id_type=pl.DeviceIdType.MESH,
-            ).start()
+        for number, place in self.team.others:
+            src = self.src if self.shared else self.src.at[number]
+            self.copy(src, self.dst.at[self.team.me], place).start()
 
     def bulk(self):
-        every = self.dst.at[pl.ds(0, len(self.others))]
-        return self.copy(every, every)
+        every = self.dst.at[pl.ds(0, self.team.size - 1)]
+        return self.copy(every, every, self.team.others[0][1])
 
     def wait_recv(self):
         self.bulk().wait_recv()
@@ -138,21 +142,15 @@
         self.bulk().wait_send()
 
 
-def signal_all(others):
+def signal_all(teams):
     sem = pltpu.get_barrier_semaphore()
-    order = [
-        (hops(axis, offset), axis, peer)
-        for axis, members in others.items()
-        for offset, peer in zip(ORDER[axis], members)
-    ]
-    for _, axis, peer in sorted(order, key=lambda item: -item[0]):
-        pl.semaphore_signal(
-            sem, inc=1, device_id={axis: peer}, device_id_type=pl.DeviceIdType.MESH
-        )
-
-
-def wait_all(others):
-    pl.semaphore_wait(pltpu.get_barrier_semaphore(), sum(map(len, others.values())))
+    order = [(far, place) for team in teams for far, (_, place) in zip(team.hops, team.others)]
+    for _, place in sorted(order, key=lambda item: -item[0]):
+        pl.semaphore_signal(sem, inc=1, device_id=place, device_id_type=pl.DeviceIdType.MESH)
+
+
+def wait_all(teams):
+    pl.semaphore_wait(pltpu.get_barrier_semaphore(), sum(team.size - 1 for team in teams))
 
 
 def step_kernel(
@@ -200,7 +198,7 @@
     send_sem,
     recv_sem,
 ):
-    me, here = lax.axis_index("grp"), lax.axis_index("region")
+    me = lax.axis_index("grp")
     cols, length = trans.shape[1], trans.shape[2]
     modes, rows, n = probe.shape[1], probe.shape[2], probe.shape[3]
     tiles = n // LANES
@@ -229,18 +227,22 @@
     ]
     for load in loads[:3]:
         load.start()
-    others = {axis: peers(axis) for axis in ("grp", "region")}
-    signal_all(others)
+    digits = {
+        name: lax.rem(lax.div(lax.axis_index(axis), unit), size)
+        for name, (axis, unit, size) in PLACE.items()
+    }
+    rows_team, plane, line = (Team(names, digits) for names in TEAMS.values())
+    signal_all((plane, line))
+    phase = [0]
+    copies = []
+
+    def exchange(src, dst, team=rows_team, shared=False):
+        at = phase[0]
+        phase[0] += 1
+        copies.append(Exchange(team, src, dst, send_sem.at[at], recv_sem.at[at], shared))
+        return copies[-1]
     loads[0].wait()
     row0, col0 = pos[0, 0], pos[0, 1]
-    phase = [0]
-    copies = []
-
-    def exchange(src, dst, axis="grp", shared=False):
-        at = phase[0]
-        phase[0] += 1
-        copies.append(Exchange(axis, others[axis], src, dst, send_sem.at[at], recv_sem.at[at], shared))
-        return copies[-1]
 
     pick = iota((n, length), 1) == iota((n, length), 0) + row0
     put[...] = pick.astype(F32).astype(BF16)
@@ -261,7 +263,7 @@
         x_send[d] = value.astype(BF16)
     x_recv[me] = x_send[me]
 
-    wait_all(others)
+    wait_all((plane, line))
     x_copy = exchange(x_send, x_recv)
     x_copy.start()
 
@@ -437,21 +439,21 @@
     )
     value = jnp.sum(totals, axis=0, keepdims=True)
     one_send[0] = value
-    one_recv[me] = value
-    one = exchange(one_send.at[0], one_recv, shared=True)
+    one_recv[plane.me] = value
+    one = exchange(one_send.at[0], one_recv, plane, shared=True)
     one.start()
     one.wait_recv()
     value = jnp.sum(one_recv[...], axis=0)
     one_send[1] = value
-    two_recv[here] = value
-    two = exchange(one_send.at[1], two_recv, "region", shared=True)
+    two_recv[line.me] = value
+    two = exchange(one_send.at[1], two_recv, line, shared=True)
     two.start()
     two.wait_recv()
     value = jnp.sum(two_recv[...], axis=0)
 
     def inner(kind, a, b):
         at = number[(kind, a, b)]
-        return value[:, at : at + 1]
+        return jnp.broadcast_to(value[:, at : at + 1], (1, LANES))
 
     curve = [
         jnp.maximum(inner("sy", i, i), CURVE_FLOOR * inner("ss", i, i)) for i in range(depth)
@@ -520,8 +522,8 @@
             pltpu.VMEM((grp, 32, LANES), BF16),
             pltpu.VMEM((grp, 32, LANES), BF16),
             pltpu.VMEM((2, 1, LANES), F32),
-            pltpu.VMEM((grp, 1, LANES), F32),
-            pltpu.VMEM((region, 1, LANES), F32),
+            pltpu.VMEM((2 * grp, 1, LANES), F32),
+            pltpu.VMEM((region // 2, 1, LANES), F32),
             pltpu.VMEM((n, grp * LANES), BF16),
             pltpu.VMEM((n, length), BF16),
             pltpu.VMEM((2, modes * rows, n), BF16),

time: 70.2 us -> 69.2 us (0.986)
  Pallas kernels: 68.7 us -> 67.6 us
    pallas_call x1, Pallas kernels: 68.7 us -> 67.6 us  [shards(): pl.pallas_call(functools.partial(step_kernel, grp, region), out_shape=(sh...]
where the time goes in v6:
time: 69.2 us; the launch traced here: 69.1 us
  Pallas kernels  67.6 us (98%)
  other arithmetic  0.79 us (1%)
    pallas_call x1, Pallas kernels, shards(): pl.pallas_call(functools.partial(step_kernel, grp, region), out_shape=(sh...  67.6 us

profile of v6, /device:TPU:1, one launch (start us, length us, event | category | flops | bytes accessed | tf_op | source)
XLA Modules:
  0.0 69.1 jit_solution(2313847270768524941)
XLA Ops:
  0.6 0.0 copy-start
  0.6 67.6 %step.1 = (f32[2,40,640]{2,1,0:T(8,128)S(1)}, f32[2,40,640]{2,1,0:T(8,128)S(1)}) custom-call(s32[1,2]{1,0:T(1,128)} %pos_hbm.1, f32[2,40,640]{2,1,0:T(8,128)} %trans_hbm.1, f32[1,32,512]{2,1,0:T(8,128)} %meas_hbm.1, bf16[2,8,32,512]{3,2,1,0:T(8,128)(2,1)} %probe_hbm.1, bf16[2,512,512]{2,1,0:T(8,128)(2,1)} %constant.4.clone.k_hbm, ...), custom_call_target="tpu_custom_call" | custom-call | tf_op jit(solution)/shard_map/step/pallas_call | solution.py:502
  68.3 0.0 copy-done
  68.3 0.8 %multiply_add_fusion = (f32[2,40,640]{2,1,0:T(8,128)}, f32[2,40,640]{2,1,0:T(8,128)}) fusion(f32[2,40,640]{2,1,0:T(8,128)S(1)} %get-tuple-element.5, f32[2,40,640]{2,1,0:T(8,128)S(1)} %copy-done, f32[2,40,640]{2,1,0:T(8,128)S(1)} %get-tuple-element.4), kind=kLoop, calls=%fused_computation | loop fusion | flops 153600 | bytes 1024000 | tf_op jit(solution)/shard_map/add | solution.py:559
Async XLA Ops:
  0.6 67.6 %copy-start = (f32[2,40,640]{2,1,0:T(8,128)S(1)}, f32[2,40,640]{2,1,0:T(8,128)}, u32[]{:S(2)}) copy-start(f32[2,40,640]{2,1,0:T(8,128)} %trans_hbm.1) | copy-start | bytes 614404

commit v7 on v6

--- a/solution.py
+++ b/solution.py
@@ -280,7 +280,7 @@
         x = x_recv[d].astype(F32)
         zero = jnp.zeros_like(x)
         stacked.append(
-            jnp.concatenate([jnp.where(first, x, zero), jnp.where(first, zero, x), zero, zero], axis=0).astype(BF16)
+            jnp.concatenate([jnp.where(first, x, zero), jnp.where(first, zero, x)], axis=0).astype(BF16)
         )
     window = jnp.transpose(dot_t(select[...], jnp.concatenate(stacked, axis=1)))
     win_r, win_i = window[:rows], window[rows : 2 * rows]
@@ -398,7 +398,7 @@
     group = iota((grp, 8, LANES), 2) // 32
     zero = jnp.zeros((grp, 8, LANES), F32)
     wide = []
-    for w in range(4):
+    for w in range((len(pieces) + 3) // 4):
         value = zero
         for p in range(4):
             if 4 * w + p < len(pieces):
@@ -519,8 +519,8 @@
             pltpu.VMEM(block, BF16),
             pltpu.VMEM(block, BF16),
             pltpu.VMEM(block, BF16),
-            pltpu.VMEM((grp, 32, LANES), BF16),
-            pltpu.VMEM((grp, 32, LANES), BF16),
+            pltpu.VMEM((grp, 24, LANES), BF16),
+            pltpu.VMEM((grp, 24, LANES), BF16),
             pltpu.VMEM((2, 1, LANES), F32),
             pltpu.VMEM((2 * grp, 1, LANES), F32),
             pltpu.VMEM((region // 2, 1, LANES), F32),

time: 69.2 us -> 69.2 us (level)
  no operation moved by 1% of the time
where the time goes in v7:
time: 69.2 us; the launch traced here: 69 us
  Pallas kernels  67.6 us (98%)
  other arithmetic  0.79 us (1%)
    pallas_call x1, Pallas kernels, shards(): pl.pallas_call(functools.partial(step_kernel, grp, region), out_shape=(sh...  67.6 us

profile of v7, /device:TPU:1, one launch (start us, length us, event | category | flops | bytes accessed | tf_op | source)
XLA Modules:
  0.0 69.0 jit_solution(17307649793135504026)
XLA Ops:
  0.6 0.0 copy-start
  0.6 67.6 %step.1 = (f32[2,40,640]{2,1,0:T(8,128)S(1)}, f32[2,40,640]{2,1,0:T(8,128)S(1)}) custom-call(s32[1,2]{1,0:T(1,128)} %pos_hbm.1, f32[2,40,640]{2,1,0:T(8,128)} %trans_hbm.1, f32[1,32,512]{2,1,0:T(8,128)} %meas_hbm.1, bf16[2,8,32,512]{3,2,1,0:T(8,128)(2,1)} %probe_hbm.1, bf16[2,512,512]{2,1,0:T(8,128)(2,1)} %constant.4.clone.k_hbm, ...), custom_call_target="tpu_custom_call" | custom-call | tf_op jit(solution)/shard_map/step/pallas_call | solution.py:502
  68.2 0.0 copy-done
  68.2 0.8 %multiply_add_fusion = (f32[2,40,640]{2,1,0:T(8,128)}, f32[2,40,640]{2,1,0:T(8,128)}) fusion(f32[2,40,640]{2,1,0:T(8,128)S(1)} %get-tuple-element.5, f32[2,40,640]{2,1,0:T(8,128)S(1)} %copy-done, f32[2,40,640]{2,1,0:T(8,128)S(1)} %get-tuple-element.4), kind=kLoop, calls=%fused_computation | loop fusion | flops 153600 | bytes 1024000 | tf_op jit(solution)/shard_map/add | solution.py:559
Async XLA Ops:
  0.6 67.6 %copy-start = (f32[2,40,640]{2,1,0:T(8,128)S(1)}, f32[2,40,640]{2,1,0:T(8,128)}, u32[]{:S(2)}) copy-start(f32[2,40,640]{2,1,0:T(8,128)} %trans_hbm.1) | copy-start | bytes 614404
